TPU v7x, 32 devices: a whole 2x2x4 slice. The times are simulated.
32 devices in a mesh: req: 8 (over z, y), grp: 4 (over x, core).
Axes of the slice: x: 2, y: 2, z: 4, core: 2. Of those that a mesh axis runs over, the one named last changes fastest.
Arguments:
- tokens: bfloat16 [128, 64, 1024], P(('req', 'grp')), may hold values from -6 to 6
- kv_pool: bfloat16 [192, 256, 2048], P('req', 'grp'), may hold values from -70 to 70
- page_table: int32 [8, 16, 6], P(None, 'grp'), may hold values from 0 to 191, as said below
- cache_lens: int32 [128], P(('req', 'grp')), may hold values from 48 to 384
- draft_lengths: int32 [8, 16], P('req'), may hold values from 32 to 64, as said below
- draft_parents: int32 [128, 64], P(('req', 'grp')), may hold values from -1 to 62, as said below
- accepted_path: int32 [128, 64], P(('req', 'grp')), may hold values from -1 to 63, as said below
- prompt_group: int32 [128], P(('req', 'grp')), may hold values from 0 to 23
- memory_kv: bfloat16 [24, 256, 2048], P(None, 'req'), may hold values from -70 to 70
- w_query: bfloat16 [1024, 1024], replicated, may hold values from -0.1875 to 0.1875
- w_key: bfloat16 [1024, 1024], replicated, may hold values from -0.1875 to 0.1875
- w_value: bfloat16 [1024, 1024], replicated, may hold values from -0.1875 to 0.1875
- w_output: bfloat16 [1024, 1024], replicated, may hold values from -0.1875 to 0.1875
- w_cross_query: bfloat16 [1024, 1024], replicated, may hold values from -0.1875 to 0.1875
- w_cross_output: bfloat16 [1024, 1024], replicated, may hold values from -0.1875 to 0.1875
- w_in: bfloat16 [1024, 4096], P(None, 'grp'), may hold values from -0.1875 to 0.1875
- w_out: bfloat16 [4096, 1024], P('grp'), may hold values from -0.09375 to 0.09375
Outputs:
- layer_out: bfloat16 [128, 64, 1024], P(('req', 'grp'))
- accepted_kv: bfloat16 [128, 64, 2048], P(('req', 'grp'))
Inputs may be any that keep to these rules, and one draw needn't show every extreme that they name: For each g < 4, the entries of page_table[:, g * 4 : (g + 1) * 4, :] name every row of kv_pool exactly once. Within one row r of page_table and one such g, at most 4 entries share the same value of e // 24, and for each g some row reaches 4. `draft_lengths`: each row sums to 704 and holds 64 at least once. `draft_parents`: position 0 has parent -1; position i >= 1 has its parent in max(0, i - 4) to i - 1. `accepted_path`: row n lists in increasing order the positions on the walk along draft_parents from one live draft position of request n back to position 0, then -1 in the remaining slots.
All inputs are finite; a program needn't handle non-finite values.
Results may differ from a plain program's by a relative error of at most 0.017.
Values may be sent and summed in bfloat16 or wider, within the bound.
A program may use at most 192 MiB of HBM per device.

v0:
```python
import jax
import jax.numpy as jnp
from jax import lax
from jax.sharding import PartitionSpec as P

HEADS = 16


EPSILON = 1e-05
NEGATIVE = -1e30


def layer_norm(values):
    center = values - jnp.mean(values, axis=-1, keepdims=True)
    spread = jnp.mean(center * center, axis=-1, keepdims=True)
    return center * lax.rsqrt(spread + EPSILON)


def ancestors(parents):
    draft_len = parents.shape[-1]
    column_ids = jnp.arange(draft_len, dtype=jnp.int32)
    linked = (parents[:, :, None] == column_ids[None, None, :]).astype(jnp.float32)
    closure = linked + jnp.eye(draft_len, dtype=jnp.float32)[None]
    for sweep_index in range(draft_len.bit_length()):
        closure = jnp.minimum(
            jnp.einsum("nij,njk->nik", closure, closure, precision=lax.Precision.HIGHEST), 1.0
        )
    return closure


def fetch_pages(kv_pool, page_table, row_index):
    owners, req_count, page_count = page_table.shape
    pool_pages, page_len, kv_width = kv_pool.shape
    capacity = pool_pages // owners + 1
    page_map = page_table.reshape(owners, pool_pages)
    source = page_map // pool_pages
    slot_ids = page_map % pool_pages
    from_here = source == row_index
    send_order = jnp.cumsum(from_here.astype(jnp.int32), axis=1) - 1
    placing = (
        from_here[:, :, None]
        & (send_order[:, :, None] == jnp.arange(capacity, dtype=jnp.int32)[None, None, :])
    ).astype(jnp.float32)
    choose = (
        slot_ids[:, :, None] == jnp.arange(pool_pages, dtype=jnp.int32)[None, None, :]
    ).astype(jnp.float32)
    select = jnp.einsum("okc,okj->ocj", placing, choose, precision=lax.Precision.HIGHEST).astype(
        jnp.bfloat16
    )
    flat_pool = kv_pool.reshape(pool_pages, page_len * kv_width)
    outgoing = jnp.dot(
        select.reshape(owners * capacity, pool_pages), flat_pool, preferred_element_type=jnp.float32
    ).astype(jnp.bfloat16)
    arrived = lax.all_to_all(
        outgoing.reshape(owners, capacity, page_len * kv_width),
        "req",
        split_axis=0,
        concat_axis=0,
        tiled=True,
    )
    my_source = lax.dynamic_index_in_dim(source, row_index, 0, keepdims=False)
    page_ids = jnp.arange(pool_pages, dtype=jnp.int32)
    earlier = (my_source[:, None] == my_source[None, :]) & (page_ids[None, :] < page_ids[:, None])
    page_rank = jnp.sum(earlier.astype(jnp.int32), axis=1)
    position = my_source * capacity + page_rank
    picking = (position[:, None] == jnp.arange(owners * capacity, dtype=jnp.int32)[None, :]).astype(
        jnp.bfloat16
    )
    gathered = jnp.dot(
        picking,
        arrived.reshape(owners * capacity, page_len * kv_width),
        preferred_element_type=jnp.float32,
    ).astype(jnp.bfloat16)
    return gathered.reshape(req_count, page_count * page_len, kv_width)


def self_attention(x_rows, cache_rows, cache_lens, parents, w_query, w_key, w_value):
    req_count, draft_len, model_width = x_rows.shape
    head_dim = model_width // HEADS
    flat_rows = x_rows.reshape(req_count * draft_len, model_width)
    query_rows = (
        jnp.dot(flat_rows, w_query, preferred_element_type=jnp.float32) * head_dim ** (-0.5)
    ).astype(jnp.bfloat16)
    key_new = jnp.dot(flat_rows, w_key, preferred_element_type=jnp.float32).astype(jnp.bfloat16)
    value_new = jnp.dot(flat_rows, w_value, preferred_element_type=jnp.float32).astype(jnp.bfloat16)
    query_heads = query_rows.reshape(req_count, draft_len, HEADS, head_dim)
    cache_keys = cache_rows[:, :, :model_width].reshape(req_count, -1, HEADS, head_dim)
    cache_values = cache_rows[:, :, model_width:].reshape(req_count, -1, HEADS, head_dim)
    new_keys = key_new.reshape(req_count, draft_len, HEADS, head_dim)
    new_values = value_new.reshape(req_count, draft_len, HEADS, head_dim)
    score_cache = jnp.einsum(
        "nihd,nphd->nhip", query_heads, cache_keys, preferred_element_type=jnp.float32
    )
    score_draft = jnp.einsum(
        "nihd,njhd->nhij", query_heads, new_keys, preferred_element_type=jnp.float32
    )
    positions = jnp.arange(cache_rows.shape[1], dtype=jnp.int32)
    score_cache = jnp.where(
        (positions[None, :] < cache_lens[:, None])[:, None, None, :], score_cache, NEGATIVE
    )
    score_draft = jnp.where((ancestors(parents) > 0.5)[:, None, :, :], score_draft, NEGATIVE)
    top_score = jnp.maximum(jnp.max(score_cache, axis=-1), jnp.max(score_draft, axis=-1))[..., None]
    expo_cache = jnp.exp(score_cache - top_score)
    expo_draft = jnp.exp(score_draft - top_score)
    expo_total = jnp.sum(expo_cache, axis=-1) + jnp.sum(expo_draft, axis=-1)
    mixed_heads = jnp.einsum(
        "nhip,nphd->nihd",
        expo_cache.astype(jnp.bfloat16),
        cache_values,
        preferred_element_type=jnp.float32,
    )
    mixed_heads = mixed_heads + jnp.einsum(
        "nhij,njhd->nihd",
        expo_draft.astype(jnp.bfloat16),
        new_values,
        preferred_element_type=jnp.float32,
    )
    mixed_heads = mixed_heads / jnp.transpose(expo_total, (0, 2, 1))[..., None]
    kv_new = jnp.concatenate([key_new, value_new], axis=1).reshape(
        req_count, draft_len, 2 * model_width
    )
    return (mixed_heads.reshape(req_count * draft_len, model_width).astype(jnp.bfloat16), kv_new)


def cross_attention(first_norm, prompt_group, memory_kv, w_cross_query, req_count, draft_len):
    model_width = first_norm.shape[1]
    head_dim = model_width // HEADS
    group_total, local_src, width_both = memory_kv.shape
    cross_query = (
        jnp.dot(first_norm, w_cross_query, preferred_element_type=jnp.float32) * head_dim ** (-0.5)
    ).astype(jnp.bfloat16)
    cross_heads = cross_query.reshape(req_count, draft_len, HEADS, head_dim)
    group_pick = (
        prompt_group[:, None] == jnp.arange(group_total, dtype=jnp.int32)[None, :]
    ).astype(jnp.bfloat16)
    top_run = jnp.full((req_count, HEADS, draft_len), NEGATIVE, jnp.float32)
    chosen = jnp.dot(
        group_pick,
        lax.all_gather(memory_kv, "req", axis=1, tiled=True).reshape(group_total, -1),
        preferred_element_type=jnp.float32,
    ).astype(jnp.bfloat16)
    chosen = chosen.reshape(req_count, -1, width_both)
    memory_keys = chosen[:, :, :model_width].reshape(req_count, -1, HEADS, head_dim)
    memory_values = chosen[:, :, model_width:].reshape(req_count, -1, HEADS, head_dim)
    scores = jnp.einsum(
        "nihd,nphd->nhip", cross_heads, memory_keys, preferred_element_type=jnp.float32
    )
    top_new = jnp.maximum(top_run, jnp.max(scores, axis=-1))
    expo_part = jnp.exp(scores - top_new[..., None])
    total_new = jnp.sum(expo_part, axis=-1)
    accum_new = jnp.einsum(
        "nhip,nphd->nhid",
        expo_part.astype(jnp.bfloat16),
        memory_values,
        preferred_element_type=jnp.float32,
    )
    mixed_heads = accum_new / total_new[..., None]
    return (
        jnp.transpose(mixed_heads, (0, 2, 1, 3))
        .reshape(req_count * draft_len, model_width)
        .astype(jnp.bfloat16)
    )


def feed_forward(input_rows, w_in, w_out):
    whole_rows = lax.all_gather(input_rows, "grp", axis=0, tiled=True)
    hidden = jax.nn.gelu(
        jnp.dot(whole_rows, w_in, preferred_element_type=jnp.float32), approximate=False
    ).astype(jnp.bfloat16)
    summed = lax.psum_scatter(
        jnp.dot(hidden, w_out, preferred_element_type=jnp.float32).astype(jnp.bfloat16),
        "grp",
        scatter_dimension=0,
        tiled=True,
    ).astype(jnp.float32)
    return layer_norm(input_rows.astype(jnp.float32) + summed).astype(jnp.bfloat16)


def per_device(
    tokens,
    kv_pool,
    page_table,
    cache_lens,
    draft_lengths,
    draft_parents,
    accepted_path,
    prompt_group,
    memory_kv,
    w_query,
    w_key,
    w_value,
    w_output,
    w_cross_query,
    w_cross_output,
    w_in,
    w_out,
):
    req_count, draft_len, model_width = tokens.shape
    row_index = lax.axis_index("req")
    col_index = lax.axis_index("grp")
    cache_rows = fetch_pages(kv_pool, page_table, row_index)
    self_mix, kv_new = self_attention(
        tokens, cache_rows, cache_lens, draft_parents, w_query, w_key, w_value
    )
    flat_rows = tokens.reshape(req_count * draft_len, model_width)
    first_norm = layer_norm(
        flat_rows.astype(jnp.float32)
        + jnp.dot(self_mix, w_output, preferred_element_type=jnp.float32)
    ).astype(jnp.bfloat16)
    cross_mix = cross_attention(
        first_norm, prompt_group, memory_kv, w_cross_query, req_count, draft_len
    )
    second_norm = layer_norm(
        first_norm.astype(jnp.float32)
        + jnp.dot(cross_mix, w_cross_output, preferred_element_type=jnp.float32)
    ).astype(jnp.bfloat16)
    group_lengths = draft_lengths[0]
    own_counts = lax.dynamic_slice_in_dim(group_lengths, col_index * req_count, req_count, 0)
    live = (jnp.arange(draft_len, dtype=jnp.int32)[None, :] < own_counts[:, None]).reshape(
        req_count * draft_len
    )
    result_rows = jnp.where(
        live[:, None], feed_forward(second_norm, w_in, w_out), jnp.zeros((), jnp.bfloat16)
    )
    path_pick = (
        accepted_path[:, :, None] == jnp.arange(draft_len, dtype=jnp.int32)[None, None, :]
    ).astype(jnp.bfloat16)
    accepted_kv = jnp.einsum(
        "nij,njc->nic", path_pick, kv_new, preferred_element_type=jnp.float32
    ).astype(jnp.bfloat16)
    return (result_rows.reshape(req_count, draft_len, model_width), accepted_kv)


def solution(mesh):
    return jax.shard_map(
        per_device,
        mesh=mesh,
        in_specs=(
            P(("req", "grp"), None, None),
            P("req", "grp", None),
            P(None, "grp", None),
            P(("req", "grp")),
            P("req", None),
            P(("req", "grp"), None),
            P(("req", "grp"), None),
            P(("req", "grp")),
            P(None, "req", None),
            P(),
            P(),
            P(),
            P(),
            P(),
            P(),
            P(None, "grp"),
            P("grp", None),
        ),
        out_specs=(P(("req", "grp"), None, None), P(("req", "grp"), None, None)),
        check_vma=False,
    )
```

profile of v0, /device:TPU:0, one launch (start us, length us, event | category | flops | bytes accessed | tf_op | source)
XLA Modules:
  0.0 732.7 jit_solution(4352914945222607861)
XLA Ops:
  10.0 8.9 %copy.66 = bf16[3,8,64,2048]{3,1,2,0:T(8,128)(2,1)} copy(bf16[3,8,64,2048]{3,2,1,0:T(8,128)(2,1)} %bitcast.80) | data formatting | bytes 12582912
  19.2 9.0 %convolution_convert_fusion.1 = bf16[32,131072]{1,0:T(8,128)(2,1)} fusion(bf16[32,24]{1,0:T(8,128)(2,1)S(1)} %bitcast.89, bf16[24,131072]{1,0:T(8,128)(2,1)} %bitcast.74), kind=kOutput, calls=%fused_computation.1 | convolution fusion | flops 205520896 | bytes 14681600 | tf_op jit(solution)/shard_map/dot_general | solution.py:51
  28.2 8.2 %reshape.228 = bf16[8,4,131072]{2,1,0:T(4,128)(2,1)} reshape(bf16[32,131072]{1,0:T(8,128)(2,1)} %convolution_convert_fusion.1) | data formatting | bytes 16777216 | tf_op jit(solution)/shard_map/reshape | solution.py:55
  36.4 7.2 all-to-all-start
  43.7 3.1 fusion.31
  46.8 1.9 reshape.232
  50.8 3.3 convolution_convert_fusion.5
  54.1 2.5 reshape.234
  56.6 3.3 convolution_convert_fusion.4
  59.8 2.5 reshape.235
  62.6 3.2 select_reduce_fusion.1
  65.9 228.8 %all-to-all-done = bf16[8,4,131072]{2,1,0:T(4,128)(2,1)} async-done(((bf16[8,4,131072]{2,1,0:T(4,128)(2,1)}), bf16[8,4,131072]{2,1,0:T(4,128)(2,1)}, u32[]{:S(2)}, u32[]{:S(2)}) %all-to-all-start) | async-done | bytes 8388640 | tf_op jit(solution)/shard_map/all_to_all | solution.py:54
  294.7 7.7 %reshape.229 = bf16[32,131072]{1,0:T(8,128)(2,1)} reshape(bf16[8,4,131072]{2,1,0:T(4,128)(2,1)} %all-to-all-done) | data formatting | bytes 16777216 | tf_op jit(solution)/shard_map/reshape | solution.py:71
  302.4 7.9 %convolution_convert_fusion.2 = bf16[24,131072]{1,0:T(8,128)(2,1)} fusion(bf16[32,131072]{1,0:T(8,128)(2,1)} %reshape.229, s32[24]{0:T(128)S(1)} %multiply_add_fusion), kind=kOutput, calls=%fused_computation.2 | convolution fusion | flops 204473088 | bytes 14680160 | tf_op jit(solution)/shard_map/dot_general | solution.py:69
  310.3 7.9 %reshape.230 = bf16[4,384,2048]{2,1,0:T(8,128)(2,1)} reshape(bf16[24,131072]{1,0:T(8,128)(2,1)} %convolution_convert_fusion.2) | data formatting | bytes 12582912 | tf_op jit(solution)/shard_map/reshape | solution.py:74
  318.2 6.2 fusion.98
  324.4 4.7 copy.52
  329.1 4.6 copy.53
  333.7 3.1 select_reduce_fusion
  337.5 2.0 fusion
  339.5 2.0 fusion.14
  341.5 1.8 fusion.22
  343.3 1.9 copy.60
  345.3 1.5 convert_element_type.114
  346.8 2.8 fusion.100
  350.6 1.7 fusion.32
  352.2 1.8 reshape.236
  354.0 236.9 %all-gather.3.cloned.1.call-done = bf16[24,256,2048]{2,1,0:T(8,128)(2,1)} async-done(((bf16[24,32,2048]{2,1,0:T(8,128)(2,1)}), bf16[24,256,2048]{2,1,0:T(8,128)(2,1)}) %all-gather.3.cloned.1.call-update) | async-done | bytes 25165840 | tf_op jit(solution)/shard_map/all_gather | solution.py:139
  590.9 26.8 %copy.67 = bf16[3,8,256,2048]{3,1,2,0:T(8,128)(2,1)} copy(bf16[3,8,256,2048]{3,2,1,0:T(8,128)(2,1)} %bitcast.73) | data formatting | bytes 50331648
  617.8 11.3 %convolution_convert_fusion = bf16[4,524288]{1,0:T(4,128)(2,1)S(1)} fusion(bf16[24,524288]{1,0:T(8,128)(2,1)} %bitcast.72, s32[4]{0:T(128)S(1)} %copy-done.9), kind=kOutput, calls=%fused_computation | convolution fusion | flops 102760544 | bytes 29360144 | tf_op jit(solution)/shard_map/dot_general | solution.py:137
  629.1 2.3 copy.88
  631.4 2.4 fusion.99
  633.9 4.0 copy.63
  637.9 4.0 copy.61
  641.8 2.5 fusion.101
  644.4 1.3 fusion.12
  645.7 1.6 fusion.21
  648.0 1.5 convert_element_type.121
  649.5 2.8 fusion.102
  652.6 1.0 multiply_convert_fusion.1
  653.7 20.2 %all-gather.5.cloned.1.call-done = bf16[1024,1024]{1,0:T(8,128)(2,1)} async-done(((bf16[256,1024]{1,0:T(8,128)(2,1)}), bf16[1024,1024]{1,0:T(8,128)(2,1)}) %all-gather.5.cloned.1.call-update) | async-done | bytes 2097168 | tf_op jit(solution)/shard_map/all_gather | solution.py:166
  673.8 15.5 %fusion.26 = bf16[1024,1024]{1,0:T(8,128)(2,1)} fusion(bf16[1024,1024]{1,0:T(8,128)(2,1)S(1)} %copy-done, bf16[1024,1024]{1,0:T(8,128)(2,1)} %all-gather.5.cloned.1.call-done, bf16[1024,1024]{1,0:T(8,128)(2,1)} %param.32), kind=kOutput, calls=%fused_computation.44 | convolution fusion | flops 4364173312 | bytes 8388608 | tf_op jit(solution)/shard_map/dot_general | solution.py:171
  689.6 1.3 pad_maximum_fusion
  690.9 1.4 convolution_convert_fusion.3
  692.4 28.6 %reduce-scatter.2.cloned.1.call-done = bf16[256,1024]{1,0:T(8,128)(2,1)} async-done(((bf16[1024,1024]{1,0:T(8,128)(2,1)}), bf16[256,1024]{1,0:T(8,128)(2,1)}) %reduce-scatter.2.cloned.1.call-update) | async-done | bytes 524304 | tf_op jit(solution)/shard_map/reduce_scatter | solution.py:170
  721.0 1.4 fusion.46
  722.3 1.4 multiply_reduce_fusion
  723.8 2.2 fusion.50
  (73 shorter events, 8.4 us)
Async XLA Ops:
  7.2 666.7 %copy-start = (bf16[1024,1024]{1,0:T(8,128)(2,1)S(1)}, bf16[1024,1024]{1,0:T(8,128)(2,1)}, u32[]{:S(2)}) copy-start(bf16[1024,1024]{1,0:T(8,128)(2,1)} %param.33) | copy-start | bytes 6291460
  7.2 583.8 %all-gather.3.cloned.1.call-start = ((), (), s32[]{:S(2)}) async-start(), calls=%async_computation.2 | async-start | bytes 28311552 | tf_op jit(solution)/shard_map/all_gather | solution.py:139
  36.4 7.3 copy-start.6
  36.4 258.3 %all-to-all-start = ((bf16[8,4,131072]{2,1,0:T(4,128)(2,1)}), bf16[8,4,131072]{2,1,0:T(4,128)(2,1)}, u32[]{:S(2)}, u32[]{:S(2)}) async-start(bf16[8,4,131072]{2,1,0:T(4,128)(2,1)} %reshape.228), calls=%async_computation | async-start | bytes 16777216 | tf_op jit(solution)/shard_map/all_to_all | solution.py:54
  43.6 5.1 copy-start.8
  43.6 630.2 %all-gather.5.cloned.1.call-start = ((), (), s32[]{:S(2)}) async-start(), calls=%async_computation.3 | async-start | bytes 2621440 | tf_op jit(solution)/shard_map/all_gather | solution.py:166
  50.8 11.8 %copy-start.10 = (s32[4]{0:T(128)S(1)}, s32[4]{0:T(128)}, u32[]{:S(2)}) copy-start(s32[4]{0:T(128)} %param.20) | copy-start | bytes 52
  333.7 3.2 copy-start.3
  336.9 2.6 copy-start.1
  339.5 2.0 copy-start.5
  346.8 3.8 copy-start.11
  349.6 1.0 copy-start.2
  590.9 26.8 %copy-start.9 = (s32[4]{0:T(128)S(1)}, s32[4]{0:T(128)}, u32[]{:S(2)}) copy-start(s32[4]{0:T(128)} %param.24) | copy-start | bytes 52
  641.8 3.9 copy-start.4
  653.6 35.8 %copy-start.12 = (s32[1,16]{1,0:T(1,128)S(1)}, s32[1,16]{1,0:T(1,128)}, u32[]{:S(2)}) copy-start(s32[1,16]{1,0:T(1,128)} %param.21) | copy-start | bytes 196
  653.6 67.3 %reduce-scatter.2.cloned.1.call-start = ((), (), s32[]{:S(2)}) async-start(), calls=%async_computation.4 | async-start | bytes 2621440 | tf_op jit(solution)/shard_map/reduce_scatter | solution.py:170
  689.3 1.6 copy-start.7
Sparse Core Ops, SparseCore 0:
  9.6 581.3 all-gather.2
  653.7 20.0 all-gather.4
  689.5 31.4 reduce-scatter.1
where the time goes:
time: 740 us; the launch traced here: 733 us
  waiting for transfers between devices  515 us (70%)
  local copies, waits for them, and re-layouts  104 us (14%)
  matrix products  78.4 us (11%)
  between operations  14.3 us (2%)
  other arithmetic  13.7 us (2%)
    all_gather x1, waiting for transfers between devices, cross_attention(): lax.all_gather(memory_kv, 'req', axis=1, tiled=True)  237 us
    all_to_all x1, waiting for transfers between devices, fetch_pages(): lax.all_to_all(outgoing.reshape(owners, capacity, page_len * kv_width), '...  229 us
    unnamed x29, local copies, waits for them, and re-layouts  38.7 us
    reduce_scatter x1, waiting for transfers between devices, feed_forward(): lax.psum_scatter(jnp.dot(hidden, w_out, preferred_element_type=jnp.float3...  28.6 us
    all_gather x1, waiting for transfers between devices, feed_forward(): whole_rows = lax.all_gather(input_rows, 'grp', axis=0, tiled=True)  20.2 us
    dot_general x1, matrix products, feed_forward(): jnp.dot(hidden, w_out, preferred_element_type=jnp.float32)  15.5 us
  transfers between devices with their start and end apart: 4, of which 4 were waited for; matrix products, arithmetic and copies ran while one was open for 15% of the time, Pallas kernels for 0%

commit v1 on v0

v1 whole, which is shorter than its diff:
```python
import jax
import jax.numpy as jnp
from jax import lax
from jax.experimental import pallas as pl
from jax.experimental.pallas import tpu as pltpu
from jax.sharding import PartitionSpec as P

HEADS = 16
BUNDLE = 4


EPSILON = 1e-05
NEGATIVE = -1e30


def layer_norm(values):
    center = values - jnp.mean(values, axis=-1, keepdims=True)
    spread = jnp.mean(center * center, axis=-1, keepdims=True)
    return center * lax.rsqrt(spread + EPSILON)


def ancestors(parents):
    draft_len = parents.shape[-1]
    column_ids = jnp.arange(draft_len, dtype=jnp.int32)
    linked = (parents[:, :, None] == column_ids[None, None, :]).astype(jnp.float32)
    closure = linked + jnp.eye(draft_len, dtype=jnp.float32)[None]
    for sweep_index in range(draft_len.bit_length()):
        half = closure.astype(jnp.bfloat16)
        closure = jnp.minimum(
            jnp.einsum("nij,njk->nik", half, half, preferred_element_type=jnp.float32), 1.0
        )
    return closure


def copy_block(ids_ref, source_ref, out_ref):
    out_ref[...] = source_ref[...]


def take_blocks(source, ids):
    count = ids.shape[0]
    block = (1,) + source.shape[1:]
    return pl.pallas_call(
        copy_block,
        grid_spec=pltpu.PrefetchScalarGridSpec(
            num_scalar_prefetch=1,
            grid=(count,),
            in_specs=[pl.BlockSpec(block, lambda step, ids_ref: (ids_ref[step], 0, 0))],
            out_specs=pl.BlockSpec(block, lambda step, ids_ref: (step, 0, 0)),
        ),
        out_shape=jax.ShapeDtypeStruct((count,) + source.shape[1:], source.dtype),
        cost_estimate=pl.CostEstimate(
            flops=0, bytes_accessed=4 * count * source[0].size, transcendentals=0
        ),
    )(ids, source)


def attend(query, keys, values, visible):
    rows, width = query.shape
    head_dim = width // HEADS
    bundle_width = BUNDLE * head_dim
    owner_row = lax.broadcasted_iota(jnp.int32, (BUNDLE * rows, bundle_width), 0) // rows
    owner_lane = lax.broadcasted_iota(jnp.int32, (BUNDLE * rows, bundle_width), 1) // head_dim
    own = owner_row == owner_lane
    if visible is not None:
        visible = jnp.concatenate([visible] * BUNDLE, axis=0)
    mixed = []
    for bundle in range(HEADS // BUNDLE):
        lanes = slice(bundle * bundle_width, (bundle + 1) * bundle_width)
        stacked = jnp.concatenate([query[:, lanes]] * BUNDLE, axis=0)
        stacked = jnp.where(own, stacked, jnp.zeros((), stacked.dtype))
        scores = lax.dot_general(
            stacked, keys[:, lanes], (((1,), (1,)), ((), ())), preferred_element_type=jnp.float32
        )
        if visible is not None:
            scores = jnp.where(visible, scores, NEGATIVE)
        expo = jnp.exp(scores - jnp.max(scores, axis=-1, keepdims=True))
        total = jnp.sum(expo, axis=-1, keepdims=True)
        mix = jnp.dot(
            expo.astype(jnp.bfloat16), values[:, lanes], preferred_element_type=jnp.float32
        )
        mix = jnp.where(own, mix / total, 0.0)
        folded = mix[:rows]
        for part in range(1, BUNDLE):
            folded = folded + mix[part * rows : (part + 1) * rows]
        mixed.append(folded.astype(jnp.bfloat16))
    return jnp.concatenate(mixed, axis=1)


def self_kernel(ids_ref, lens_ref, query_ref, key_ref, value_ref, reach_ref, *rest):
    page_refs, out_ref = rest[:-1], rest[-1]
    request = pl.program_id(0)
    width = query_ref.shape[1]
    rows = query_ref.shape[0]
    context = sum(ref.shape[1] for ref in page_refs)
    keys = jnp.concatenate([ref[0, :, :width] for ref in page_refs] + [key_ref[...]], axis=0)
    values = jnp.concatenate([ref[0, :, width:] for ref in page_refs] + [value_ref[...]], axis=0)
    positions = lax.broadcasted_iota(jnp.int32, (rows, context), 1)
    cached = jnp.where(positions < lens_ref[request], 1.0, 0.0)
    visible = jnp.concatenate([cached, reach_ref[0]], axis=1) > 0.5
    out_ref[...] = attend(query_ref[...], keys, values, visible)


def self_attention(query, key_new, value_new, pages, page_ids, cache_lens, reach):
    req_count, draft_len, _ = reach.shape
    width = query.shape[1]
    page_count = page_ids.shape[0] // req_count
    page_block = (1,) + pages.shape[1:]
    row_spec = pl.BlockSpec((draft_len, width), lambda n, ids, lens: (n, 0))

    def page_spec(place):
        return pl.BlockSpec(page_block, lambda n, ids, lens: (ids[n * page_count + place], 0, 0))

    keys_total = page_count * pages.shape[1] + draft_len
    return pl.pallas_call(
        self_kernel,
        grid_spec=pltpu.PrefetchScalarGridSpec(
            num_scalar_prefetch=2,
            grid=(req_count,),
            in_specs=[
                row_spec,
                row_spec,
                row_spec,
                pl.BlockSpec((1, draft_len, draft_len), lambda n, ids, lens: (n, 0, 0)),
            ]
            + [page_spec(place) for place in range(page_count)],
            out_specs=row_spec,
        ),
        out_shape=jax.ShapeDtypeStruct(query.shape, jnp.bfloat16),
        cost_estimate=pl.CostEstimate(
            flops=4 * BUNDLE * query.shape[0] * keys_total * width,
            bytes_accessed=4 * req_count * keys_total * width + 8 * query.size,
            transcendentals=query.shape[0] * keys_total * HEADS,
        ),
    )(page_ids, cache_lens, query, key_new, value_new, reach, *([pages] * page_count))


def cross_kernel(query_ref, memory_ref, out_ref):
    width = query_ref.shape[1]
    positions = memory_ref.shape[0] * memory_ref.shape[2]
    keys = memory_ref[:, 0, :, :width].reshape(positions, width)
    values = memory_ref[:, 0, :, width:].reshape(positions, width)
    out_ref[...] = attend(query_ref[...], keys, values, None)


def cross_attention(query, memory):
    owners, req_count, local_src, width_both = memory.shape
    rows, width = query.shape
    draft_len = rows // req_count
    row_spec = pl.BlockSpec((draft_len, width), lambda n: (n, 0))
    return pl.pallas_call(
        cross_kernel,
        grid=(req_count,),
        in_specs=[
            row_spec,
            pl.BlockSpec((owners, 1, local_src, width_both), lambda n: (0, n, 0, 0)),
        ],
        out_specs=row_spec,
        out_shape=jax.ShapeDtypeStruct(query.shape, jnp.bfloat16),
        cost_estimate=pl.CostEstimate(
            flops=4 * BUNDLE * rows * owners * local_src * width,
            bytes_accessed=2 * memory.size + 4 * query.size,
            transcendentals=rows * owners * local_src * HEADS,
        ),
    )(query, memory)


def page_plan(page_table, pool_pages, row_index):
    owners = page_table.shape[0]
    capacity = pool_pages // owners + 1
    page_map = page_table.reshape(owners, -1)
    source = page_map // pool_pages
    slot_ids = page_map % pool_pages
    from_here = source == row_index
    send_order = jnp.cumsum(from_here.astype(jnp.int32), axis=1) - 1
    slots = jnp.arange(capacity, dtype=jnp.int32)
    placing = from_here[:, :, None] & (send_order[:, :, None] == slots[None, None, :])
    send_ids = jnp.sum(jnp.where(placing, slot_ids[:, :, None], 0), axis=1).reshape(-1)
    my_source = lax.dynamic_index_in_dim(source, row_index, 0, keepdims=False)
    page_ids = jnp.arange(page_map.shape[1], dtype=jnp.int32)
    earlier = (my_source[:, None] == my_source[None, :]) & (page_ids[None, :] < page_ids[:, None])
    page_rank = jnp.sum(earlier.astype(jnp.int32), axis=1)
    return send_ids, my_source * capacity + page_rank


def exchange(packed, owners):
    shaped = packed.reshape((owners, packed.shape[0] // owners) + packed.shape[1:])
    return lax.all_to_all(shaped, "req", split_axis=0, concat_axis=0, tiled=True)


def per_device(
    tokens,
    kv_pool,
    page_table,
    cache_lens,
    draft_lengths,
    draft_parents,
    accepted_path,
    prompt_group,
    memory_kv,
    w_query,
    w_key,
    w_value,
    w_output,
    w_cross_query,
    w_cross_output,
    w_in,
    w_out,
):
    req_count, draft_len, model_width = tokens.shape
    owners = page_table.shape[0]
    head_dim = model_width // HEADS
    scale = head_dim ** (-0.5)
    row_index = lax.axis_index("req")
    col_index = lax.axis_index("grp")
    all_groups = lax.all_gather(prompt_group, "req", axis=0, tiled=True)
    w_in_full = lax.all_gather(w_in, "grp", axis=0, tiled=False)
    w_out_full = lax.all_gather(w_out, "grp", axis=0, tiled=True)
    send_ids, page_ids = page_plan(page_table, kv_pool.shape[0], row_index)
    pages = exchange(take_blocks(kv_pool, send_ids), owners)
    pages = pages.reshape((-1,) + kv_pool.shape[1:])
    memory = exchange(take_blocks(memory_kv, all_groups), owners)

    flat_rows = tokens.reshape(req_count * draft_len, model_width)
    query_rows = (jnp.dot(flat_rows, w_query, preferred_element_type=jnp.float32) * scale).astype(
        jnp.bfloat16
    )
    key_new = jnp.dot(flat_rows, w_key, preferred_element_type=jnp.float32).astype(jnp.bfloat16)
    value_new = jnp.dot(flat_rows, w_value, preferred_element_type=jnp.float32).astype(jnp.bfloat16)
    reach = ancestors(draft_parents)
    path_pick = (
        accepted_path[:, :, None] == jnp.arange(draft_len, dtype=jnp.int32)[None, None, :]
    ).astype(jnp.bfloat16)
    accepted_kv = jnp.concatenate(
        [
            jnp.einsum(
                "nij,njc->nic",
                path_pick,
                part.reshape(req_count, draft_len, model_width),
                preferred_element_type=jnp.float32,
            ).astype(jnp.bfloat16)
            for part in (key_new, value_new)
        ],
        axis=2,
    )
    self_mix = self_attention(query_rows, key_new, value_new, pages, page_ids, cache_lens, reach)
    first_norm = layer_norm(
        flat_rows.astype(jnp.float32)
        + jnp.dot(self_mix, w_output, preferred_element_type=jnp.float32)
    ).astype(jnp.bfloat16)
    cross_query = (
        jnp.dot(first_norm, w_cross_query, preferred_element_type=jnp.float32) * scale
    ).astype(jnp.bfloat16)
    cross_mix = cross_attention(cross_query, memory)
    second_norm = layer_norm(
        first_norm.astype(jnp.float32)
        + jnp.dot(cross_mix, w_cross_output, preferred_element_type=jnp.float32)
    ).astype(jnp.bfloat16)
    summed = jnp.zeros(second_norm.shape, jnp.float32)
    hidden = [
        jax.nn.gelu(
            jnp.dot(second_norm, w_in_full[part], preferred_element_type=jnp.float32),
            approximate=False,
        ).astype(jnp.bfloat16)
        for part in range(w_in_full.shape[0])
    ]
    summed = jnp.dot(
        jnp.concatenate(hidden, axis=1), w_out_full, preferred_element_type=jnp.float32
    )
    group_lengths = draft_lengths[0]
    own_counts = lax.dynamic_slice_in_dim(group_lengths, col_index * req_count, req_count, 0)
    live = (jnp.arange(draft_len, dtype=jnp.int32)[None, :] < own_counts[:, None]).reshape(
        req_count * draft_len
    )
    normed = layer_norm(second_norm.astype(jnp.float32) + summed).astype(jnp.bfloat16)
    result_rows = jnp.where(live[:, None], normed, jnp.zeros((), jnp.bfloat16))
    return (result_rows.reshape(req_count, draft_len, model_width), accepted_kv)


def solution(mesh):
    return jax.shard_map(
        per_device,
        mesh=mesh,
        in_specs=(
            P(("req", "grp"), None, None),
            P("req", "grp", None),
            P(None, "grp", None),
            P(("req", "grp")),
            P("req", None),
            P(("req", "grp"), None),
            P(("req", "grp"), None),
            P(("req", "grp")),
            P(None, "req", None),
            P(),
            P(),
            P(),
            P(),
            P(),
            P(),
            P(None, "grp"),
            P("grp", None),
        ),
        out_specs=(P(("req", "grp"), None, None), P(("req", "grp"), None, None)),
        check_vma=False,
    )
```

time: 740 us -> 378 us (0.51)
  waiting for transfers between devices: 515 us -> 71.9 us
  blocking collectives: 0 us -> 181 us
  local copies, waits for them, and re-layouts: 104 us -> 3.09 us
  Pallas kernels: 0 us -> 52.1 us
  matrix products: 78.4 us -> 35.9 us
  other arithmetic: 13.7 us -> 5.82 us
    all_gather x2, waiting for transfers between devices: 257 us -> 0.02 us  [the longest x1 0.02 us: per_device(): w_in_full = lax.all_gather(w_in, 'grp', axis=0, tiled=False)]
    unnamed x0 -> x1, blocking collectives: none -> 181 us
    all_to_all x1 -> x2, waiting for transfers between devices: 229 us -> 70.5 us  [exchange(): lax.all_to_all(shaped, 'req', split_axis=0, concat_axis=0, tiled=True)]
    pallas_call x0 -> x4, Pallas kernels: none -> 52.1 us  [the longest x2 38.4 us: take_blocks(): pl.pallas_call(copy_block, grid_spec=pltpu.PrefetchScalarGridSpec(num_sca...]
    dot_general x23 -> x15, matrix products: 72.8 us -> 31.1 us  [the longest x4 15.9 us: per_device(): jnp.dot(second_norm, w_in_full[part], preferred_element_type=jnp.float32)]
    unnamed x29 -> x31, local copies, waits for them, and re-layouts: 38.7 us -> 1.65 us
    reshape x7 -> x1, local copies, waits for them, and re-layouts: 32.5 us -> 0.6 us  [page_plan(): jnp.sum(jnp.where(placing, slot_ids[:, :, None], 0), axis=1).reshape(-1)]
    reduce_scatter x1 -> x0, waiting for transfers between devices: 28.6 us -> none  [feed_forward(): lax.psum_scatter(jnp.dot(hidden, w_out, preferred_element_type=jnp.float3...]
  transfers between devices with their start and end apart: 4 -> 4, of which waited for: 4 -> 1; matrix products, arithmetic and copies ran while one was open for 15% -> 9% of each run, Pallas kernels for 0% -> 9%
where the time goes in v1:
time: 378 us; the launch traced here: 377 us
  blocking collectives  181 us (48%)
  waiting for transfers between devices  71.9 us (19%)
  Pallas kernels  52.1 us (14%)
  matrix products  35.9 us (9%)
  between operations  15 us (4%)
  starting transfers between devices  12.1 us (3%)
  other arithmetic  5.82 us (2%)
    unnamed x1, blocking collectives  181 us
    all_to_all x2, waiting for transfers between devices, exchange(): lax.all_to_all(shaped, 'req', split_axis=0, concat_axis=0, tiled=True)  70.5 us
    pallas_call x2, Pallas kernels, take_blocks(): pl.pallas_call(copy_block, grid_spec=pltpu.PrefetchScalarGridSpec(num_sca...  38.4 us
    dot_general x4, matrix products, per_device(): jnp.dot(second_norm, w_in_full[part], preferred_element_type=jnp.float32)  15.9 us
    all_to_all x2, starting transfers between devices, exchange(): lax.all_to_all(shaped, 'req', split_axis=0, concat_axis=0, tiled=True)  12 us
    pallas_call x1, Pallas kernels, self_attention(): pl.pallas_call(self_kernel, grid_spec=pltpu.PrefetchScalarGridSpec(num_sc...  7.72 us
  transfers between devices with their start and end apart: 4, of which 1 were waited for; matrix products, arithmetic and copies ran while one was open for 9% of the time, Pallas kernels for 9%

profile of v1, /device:TPU:0, one launch (start us, length us, event | category | flops | bytes accessed | tf_op | source)
XLA Modules:
  0.0 376.8 jit_solution(16002234671828652853)
XLA Ops:
  7.2 0.9 broadcast_remainder_fusion
  8.1 0.7 sign_compare_fusion
  8.8 0.1 copy.26
  9.0 0.1 copy.27
  9.2 0.1 copy.25
  9.3 0.1 ne.50
  9.4 0.2 reduce_window_sum.11
  9.6 0.1 select_reduce_fusion
  9.8 0.6 reshape.154.ids_ref
  10.4 19.9 %shard_map.176 = bf16[32,64,2048]{2,1,0:T(8,128)(2,1)} custom-call(s32[32]{0:T(128)} %reshape.154.ids_ref, bf16[24,64,2048]{2,1,0:T(8,128)(2,1)} %source_ref.2), custom_call_target="tpu_custom_call" | custom-call | bytes 16777216 | tf_op jit(solution)/shard_map/pallas_call | solution.py:42
  30.3 7.2 %all-to-all-start = ((bf16[8,4,64,2048]{3,2,1,0:T(8,128)(2,1)}), bf16[8,4,64,2048]{3,2,1,0:T(8,128)(2,1)}, u32[]{:S(2)}, u32[]{:S(2)}) async-start(bf16[8,4,64,2048]{3,2,1,0:T(8,128)(2,1)} %bitcast.38), calls=%async_computation | async-start | bytes 16777216 | tf_op jit(solution)/shard_map/all_to_all | solution.py:187
  37.6 0.7 all-gather.6.cloned.1.call-update
  38.4 0.7 all-gather.4.cloned.1.call-update
  39.1 0.6 dynamic-slice.1
  40.4 0.2 dynamic-update-slice
  40.6 180.9 %all-reduce.ids_ref = s32[32]{0:T(128)} all-reduce(s32[32]{0:T(128)S(1)} %dynamic-update-slice), channel_id=1, replica_groups=mesh['req'=8,'grp'=4] {'req'}, use_global_device_ids=true, to_apply=%add | all-reduce | flops 32 | bytes 256
  221.5 18.5 %shard_map.178 = bf16[32,32,2048]{2,1,0:T(8,128)(2,1)} custom-call(s32[32]{0:T(128)} %all-reduce.ids_ref, bf16[24,32,2048]{2,1,0:T(8,128)(2,1)} %source_ref.3), custom_call_target="tpu_custom_call" | custom-call | bytes 8388608 | tf_op jit(solution)/shard_map/pallas_call | solution.py:42
  240.0 4.7 %all-to-all-start.1 = ((bf16[8,4,32,2048]{3,2,1,0:T(8,128)(2,1)}), bf16[8,4,32,2048]{3,2,1,0:T(8,128)(2,1)}, u32[]{:S(2)}, u32[]{:S(2)}) async-start(bf16[8,4,32,2048]{3,2,1,0:T(8,128)(2,1)} %bitcast.39), calls=%async_computation.1 | async-start | bytes 8388608 | tf_op jit(solution)/shard_map/all_to_all | solution.py:187
  244.9 0.1 lt.53
  245.0 0.2 convert_reduce_fusion
  245.2 0.6 multiply_add_fusion.ids_ref
  245.8 0.5 fusion.22
  246.3 0.3 fusion.24
  246.6 0.3 fusion.26
  246.9 0.8 convolution_minimum_fusion.reach_ref
  247.7 2.4 convolution_convert_fusion.2.value_ref
  250.2 0.3 convolution_convert_fusion
  250.5 0.7 convolution_convert_fusion.3.key_ref
  251.3 0.3 convolution_convert_fusion.1
  251.6 1.1 pad_maximum_fusion
  252.7 0.7 copy-done.8
  253.4 1.5 fusion.19.query_ref
  255.0 7.7 %shard_map.177 = bf16[256,1024]{1,0:T(8,128)(2,1)} custom-call(s32[24]{0:T(128)} %multiply_add_fusion.ids_ref, s32[4]{0:T(128)} %lens_ref.1, bf16[256,1024]{1,0:T(8,128)(2,1)} %fusion.19.query_ref, bf16[256,1024]{1,0:T(8,128)(2,1)} %copy-done.3, bf16[256,1024]{1,0:T(8,128)(2,1)} %copy-done.2, f32[4,64,64]{2,1,0:T(8,128)} %convolution_minimum_fusion.reach_ref, ...), custom_call_target="tpu_custom_call" | custom-call | flops 1879048192 | bytes 9437184 | tf_op jit(solution)/shard_map/pallas_call | solution.py:114
  262.7 2.1 fusion.93
  264.8 0.3 multiply_reduce_fusion.2
  265.1 1.6 fusion.20.query_ref
  266.7 70.5 %all-to-all-done.1.memory_ref = bf16[8,4,32,2048]{3,2,1,0:T(8,128)(2,1)} async-done(((bf16[8,4,32,2048]{3,2,1,0:T(8,128)(2,1)}), bf16[8,4,32,2048]{3,2,1,0:T(8,128)(2,1)}, u32[]{:S(2)}, u32[]{:S(2)}) %all-to-all-start.1) | async-done | bytes 4194336 | tf_op jit(solution)/shard_map/all_to_all | solution.py:187
  337.2 6.0 %shard_map.179 = bf16[256,1024]{1,0:T(8,128)(2,1)} custom-call(bf16[256,1024]{1,0:T(8,128)(2,1)} %fusion.20.query_ref, bf16[8,4,32,2048]{3,2,1,0:T(8,128)(2,1)} %all-to-all-done.1.memory_ref), custom_call_target="tpu_custom_call" | custom-call | flops 1073741824 | bytes 5242880 | tf_op jit(solution)/shard_map/pallas_call | solution.py:150
  343.2 2.6 fusion.94
  345.8 0.3 multiply_reduce_fusion.1
  346.1 0.2 multiply_convert_fusion.1
  346.3 4.6 %fusion.29 = bf16[256,1024]{1,0:T(8,128)(2,1)S(1)} fusion(bf16[256,1024]{1,0:T(8,128)(2,1)S(1)} %multiply_convert_fusion.1, bf16[4096,1024]{1,0:T(8,128)(2,1)} %all-gather.6.cloned.1.call-done), kind=kOutput, calls=%fused_computation.46 | convolution fusion | flops 553910272 | bytes 3145728 | tf_op jit(solution)/shard_map/dot_general | solution.py:261
  350.9 3.8 %fusion.32 = bf16[256,1024]{1,0:T(8,128)(2,1)} fusion(bf16[256,1024]{1,0:T(8,128)(2,1)S(1)} %multiply_convert_fusion.1, bf16[4096,1024]{1,0:T(8,128)(2,1)S(1)} %copy-done.6), kind=kOutput, calls=%fused_computation.49 | convolution fusion | flops 553910272 | bytes 3145728 | tf_op jit(solution)/shard_map/dot_general | solution.py:261
  354.7 3.8 %fusion.35 = bf16[256,1024]{1,0:T(8,128)(2,1)} fusion(bf16[256,1024]{1,0:T(8,128)(2,1)S(1)} %multiply_convert_fusion.1, bf16[4096,1024]{1,0:T(8,128)(2,1)S(1)} %copy-done.6), kind=kOutput, calls=%fused_computation.52 | convolution fusion | flops 553910272 | bytes 3145728 | tf_op jit(solution)/shard_map/dot_general | solution.py:261
  358.5 3.7 fusion.38
  362.2 6.4 %fusion.95 = (f32[256]{0:T(256)S(1)}, f32[256,1024]{1,0:T(8,128)S(1)}) fusion(bf16[4096,1024]{1,0:T(8,128)(2,1)} %all-gather.4.cloned.1.call-done, bf16[256,1024]{1,0:T(8,128)(2,1)} %fusion.38, bf16[256,1024]{1,0:T(8,128)(2,1)} %fusion.35, bf16[256,1024]{1,0:T(8,128)(2,1)} %fusion.32, bf16[256,1024]{1,0:T(8,128)(2,1)S(1)} %fusion.29, ...), kind=kOutput, calls=%fused_computation.167 | convolution fusion | flops 2156658432 | bytes 12059648 | tf_op jit(solution)/shard_map/dot_general | solution.py:266
  368.7 0.3 multiply_reduce_fusion
  368.9 1.0 fusion.75
  (49 shorter events, 0.6 us)
Async XLA Ops:
  7.2 255.5 %copy-start = (bf16[1024,1024]{1,0:T(8,128)(2,1)S(1)}, bf16[1024,1024]{1,0:T(8,128)(2,1)}, u32[]{:S(2)}) copy-start(bf16[1024,1024]{1,0:T(8,128)(2,1)} %param.29) | copy-start | bytes 6291460
  30.3 209.7 %all-to-all-start = ((bf16[8,4,64,2048]{3,2,1,0:T(8,128)(2,1)}), bf16[8,4,64,2048]{3,2,1,0:T(8,128)(2,1)}, u32[]{:S(2)}, u32[]{:S(2)}) async-start(bf16[8,4,64,2048]{3,2,1,0:T(8,128)(2,1)} %bitcast.38), calls=%async_computation | async-start | bytes 16777216 | tf_op jit(solution)/shard_map/all_to_all | solution.py:187
  37.6 1.5 copy-start.13
  37.6 2.8 copy-start.11
  37.6 308.7 %all-gather.6.cloned.1.call-start = ((), (), s32[]{:S(2)}) async-start(), calls=%async_computation.3 | async-start | bytes 10485760 | tf_op jit(solution)/shard_map/all_gather | solution.py:216
  38.3 323.9 %all-gather.4.cloned.1.call-start = ((), (), s32[]{:S(2)}) async-start(), calls=%async_computation.2 | async-start | bytes 10485760 | tf_op jit(solution)/shard_map/all_gather | solution.py:217
  240.0 4.8 %copy-start.12 = (s32[1,16]{1,0:T(1,128)S(1)}, s32[1,16]{1,0:T(1,128)}, u32[]{:S(2)}) copy-start(s32[1,16]{1,0:T(1,128)} %param.21) | copy-start | bytes 196
  240.0 5.8 %copy-start.10 = (s32[4,64]{1,0:T(4,128)S(1)}, s32[4,64]{1,0:T(4,128)}, u32[]{:S(2)}) copy-start(s32[4,64]{1,0:T(4,128)} %param.22) | copy-start | bytes 3076
  240.0 7.7 %copy-start.4 = (bf16[4,64,1024]{2,1,0:T(8,128)(2,1)S(1)}, bf16[4,64,1024]{2,1,0:T(8,128)(2,1)}, u32[]{:S(2)}) copy-start(bf16[4,64,1024]{2,1,0:T(8,128)(2,1)} %param.17) | copy-start | bytes 1572868
  240.0 97.2 %all-to-all-start.1 = ((bf16[8,4,32,2048]{3,2,1,0:T(8,128)(2,1)}), bf16[8,4,32,2048]{3,2,1,0:T(8,128)(2,1)}, u32[]{:S(2)}, u32[]{:S(2)}) async-start(bf16[8,4,32,2048]{3,2,1,0:T(8,128)(2,1)} %bitcast.39), calls=%async_computation.1 | async-start | bytes 8388608 | tf_op jit(solution)/shard_map/all_to_all | solution.py:187
  246.3 3.9 %copy-start.5 = (s32[4,64]{1,0:T(4,128)S(1)}, s32[4,64]{1,0:T(4,128)}, u32[]{:S(2)}) copy-start(s32[4,64]{1,0:T(4,128)} %param.23) | copy-start | bytes 3076
  247.7 2.8 copy-start.7
  250.1 1.1 copy-start.2
  251.3 3.7 copy-start.3
  251.3 2.2 copy-start.8
  262.7 2.4 copy-start.9
  346.3 4.6 %copy-start.6 = (bf16[4096,1024]{1,0:T(8,128)(2,1)S(1)}, bf16[4096,1024]{1,0:T(8,128)(2,1)}, u32[]{:S(2)}) copy-start(bf16[4096,1024]{1,0:T(8,128)(2,1)} %all-gather.6.cloned.1.call-done) | copy-start | bytes 25165828
  362.2 7.7 %copy-start.1 = (bf16[1024,1024]{1,0:T(8,128)(2,1)S(1)}, bf16[1024,1024]{1,0:T(8,128)(2,1)}, u32[]{:S(2)}) copy-start(bf16[1024,1024]{1,0:T(8,128)(2,1)} %param.29) | copy-start | bytes 6291460
Sparse Core Ops, SparseCore 0:
  40.0 59.7 all-gather.5
  101.4 58.2 all-gather.3

commit v2 on v1

--- a/solution.py
+++ b/solution.py
@@ -1,3 +1,5 @@
+import functools
+
 import jax
 import jax.numpy as jnp
 from jax import lax
@@ -32,24 +34,66 @@
     return closure
 
 
-def copy_block(ids_ref, source_ref, out_ref):
-    out_ref[...] = source_ref[...]
+def pack_kernel(count, ids_ref, source_ref, out_ref, sems):
+    copies = [
+        pltpu.make_async_copy(source_ref.at[ids_ref[slot]], out_ref.at[slot], sems.at[slot])
+        for slot in range(count)
+    ]
+    for copy in copies:
+        copy.start()
+    for copy in copies:
+        copy.wait()
 
 
 def take_blocks(source, ids):
     count = ids.shape[0]
-    block = (1,) + source.shape[1:]
     return pl.pallas_call(
-        copy_block,
-        grid_spec=pltpu.PrefetchScalarGridSpec(
-            num_scalar_prefetch=1,
-            grid=(count,),
-            in_specs=[pl.BlockSpec(block, lambda step, ids_ref: (ids_ref[step], 0, 0))],
-            out_specs=pl.BlockSpec(block, lambda step, ids_ref: (step, 0, 0)),
-        ),
+        functools.partial(pack_kernel, count),
+        in_specs=[
+            pl.BlockSpec(memory_space=pltpu.SMEM),
+            pl.BlockSpec(memory_space=pl.ANY),
+        ],
+        out_specs=pl.BlockSpec(memory_space=pl.ANY),
         out_shape=jax.ShapeDtypeStruct((count,) + source.shape[1:], source.dtype),
+        scratch_shapes=[pltpu.SemaphoreType.DMA((count,))],
         cost_estimate=pl.CostEstimate(
             flops=0, bytes_accessed=4 * count * source[0].size, transcendentals=0
+        ),
+    )(ids, source)
+
+
+def prompt_pack_kernel(parts, slots, ids_ref, source_ref, *rest):
+    out_refs, sems = rest[:parts], rest[parts]
+    copies = [
+        pltpu.make_async_copy(
+            source_ref.at[:, ids_ref[part * slots + slot]],
+            out_refs[part].at[slot],
+            sems.at[part * slots + slot],
+        )
+        for part in range(parts)
+        for slot in range(slots)
+    ]
+    for copy in copies:
+        copy.start()
+    for copy in copies:
+        copy.wait()
+
+
+def take_prompts(source, ids, parts):
+    owners, _, rows, width = source.shape
+    slots = ids.shape[0] // parts
+    shape = jax.ShapeDtypeStruct((slots, owners, rows, width), source.dtype)
+    return pl.pallas_call(
+        functools.partial(prompt_pack_kernel, parts, slots),
+        in_specs=[
+            pl.BlockSpec(memory_space=pltpu.SMEM),
+            pl.BlockSpec(memory_space=pl.ANY),
+        ],
+        out_specs=[pl.BlockSpec(memory_space=pl.ANY)] * parts,
+        out_shape=[shape] * parts,
+        scratch_shapes=[pltpu.SemaphoreType.DMA((parts * slots,))],
+        cost_estimate=pl.CostEstimate(
+            flops=0, bytes_accessed=4 * parts * shape.size, transcendentals=0
         ),
     )(ids, source)
 
@@ -134,34 +178,66 @@
     )(page_ids, cache_lens, query, key_new, value_new, reach, *([pages] * page_count))
 
 
-def cross_kernel(query_ref, memory_ref, out_ref):
+def cross_kernel(query_ref, *rest):
+    memory_refs, out_ref = rest[:-1], rest[-1]
     width = query_ref.shape[1]
-    positions = memory_ref.shape[0] * memory_ref.shape[2]
-    keys = memory_ref[:, 0, :, :width].reshape(positions, width)
-    values = memory_ref[:, 0, :, width:].reshape(positions, width)
-    out_ref[...] = attend(query_ref[...], keys, values, None)
-
-
-def cross_attention(query, memory):
-    owners, req_count, local_src, width_both = memory.shape
+
+    def joined(lanes):
+        return jnp.concatenate(
+            [
+                ref[0, block, :, lanes]
+                for ref in memory_refs
+                for block in range(ref.shape[1])
+            ],
+            axis=0,
+        )
+
+    out_ref[...] = attend(
+        query_ref[...], joined(slice(0, width)), joined(slice(width, 2 * width)), None
+    )
+
+
+def cross_attention(query, memory_parts):
+    req_count = memory_parts[0].shape[0]
     rows, width = query.shape
     draft_len = rows // req_count
     row_spec = pl.BlockSpec((draft_len, width), lambda n: (n, 0))
+    memory_size = sum(part.size for part in memory_parts)
     return pl.pallas_call(
         cross_kernel,
         grid=(req_count,),
-        in_specs=[
-            row_spec,
-            pl.BlockSpec((owners, 1, local_src, width_both), lambda n: (0, n, 0, 0)),
-        ],
+        in_specs=[row_spec]
+        + [pl.BlockSpec((1,) + part.shape[1:], lambda n: (n, 0, 0, 0)) for part in memory_parts],
         out_specs=row_spec,
         out_shape=jax.ShapeDtypeStruct(query.shape, jnp.bfloat16),
         cost_estimate=pl.CostEstimate(
-            flops=4 * BUNDLE * rows * owners * local_src * width,
-            bytes_accessed=2 * memory.size + 4 * query.size,
-            transcendentals=rows * owners * local_src * HEADS,
-        ),
-    )(query, memory)
+            flops=2 * BUNDLE * draft_len * memory_size,
+            bytes_accessed=2 * memory_size + 4 * query.size,
+            transcendentals=HEADS * draft_len * memory_size // (2 * width),
+        ),
+    )(query, *memory_parts)
+
+
+def fetch_prompts(memory_kv):
+    columns = lax.axis_size("grp")
+    col_index = lax.axis_index("grp")
+    share = memory_kv.shape[1] // columns
+    quarter = lax.dynamic_slice_in_dim(memory_kv, col_index * share, share, 1)
+    return lax.all_gather(quarter, "req", axis=0, tiled=False)
+
+
+def trade_prompts(gathered, column_groups):
+    columns = lax.axis_size("grp")
+    col_index = lax.axis_index("grp")
+    rolled = lax.dynamic_slice_in_dim(
+        jnp.concatenate([column_groups, column_groups], axis=0), col_index, columns, 0
+    )
+    packed = take_prompts(gathered, rolled.reshape(-1), columns)
+    arrived = [packed[0]]
+    for shift in range(1, columns):
+        ring = [(column, (column + shift) % columns) for column in range(columns)]
+        arrived.append(lax.ppermute(packed[shift], "grp", ring))
+    return arrived
 
 
 def page_plan(page_table, pool_pages, row_index):
@@ -212,13 +288,25 @@
     scale = head_dim ** (-0.5)
     row_index = lax.axis_index("req")
     col_index = lax.axis_index("grp")
-    all_groups = lax.all_gather(prompt_group, "req", axis=0, tiled=True)
+    send_ids, page_ids = page_plan(page_table, kv_pool.shape[0], row_index)
+    shared = memory_kv.shape[1] // lax.axis_size("grp") >= 8
+    if shared:
+        column_groups = lax.all_gather(prompt_group, "grp", axis=0, tiled=False)
+        send_ids, column_groups = lax.optimization_barrier((send_ids, column_groups))
+        gathered = fetch_prompts(memory_kv)
+        packed, w_in, w_out = lax.optimization_barrier(
+            (take_blocks(kv_pool, send_ids), w_in, w_out)
+        )
+        pages = exchange(packed, owners)
+        memory_parts = trade_prompts(gathered, column_groups)
+    else:
+        all_groups = lax.all_gather(prompt_group, "req", axis=0, tiled=True)
+        pages = exchange(take_blocks(kv_pool, send_ids), owners)
+        memory = exchange(take_blocks(memory_kv, all_groups), owners)
+        memory_parts = [jnp.transpose(memory, (1, 0, 2, 3))]
+    pages = pages.reshape((-1,) + kv_pool.shape[1:])
     w_in_full = lax.all_gather(w_in, "grp", axis=0, tiled=False)
     w_out_full = lax.all_gather(w_out, "grp", axis=0, tiled=True)
-    send_ids, page_ids = page_plan(page_table, kv_pool.shape[0], row_index)
-    pages = exchange(take_blocks(kv_pool, send_ids), owners)
-    pages = pages.reshape((-1,) + kv_pool.shape[1:])
-    memory = exchange(take_blocks(memory_kv, all_groups), owners)
 
     flat_rows = tokens.reshape(req_count * draft_len, model_width)
     query_rows = (jnp.dot(flat_rows, w_query, preferred_element_type=jnp.float32) * scale).astype(
@@ -250,7 +338,7 @@
     cross_query = (
         jnp.dot(first_norm, w_cross_query, preferred_element_type=jnp.float32) * scale
     ).astype(jnp.bfloat16)
-    cross_mix = cross_attention(cross_query, memory)
+    cross_mix = cross_attention(cross_query, memory_parts)
     second_norm = layer_norm(
         first_norm.astype(jnp.float32)
         + jnp.dot(cross_mix, w_cross_output, preferred_element_type=jnp.float32)

time: 378 us -> 517 us (1.37)
  Pallas kernels: 52.1 us -> 399 us
  blocking collectives: 181 us -> 6.35 us
  waiting for transfers between devices: 71.9 us -> 39.9 us
    pallas_call x3, Pallas kernels: 44.4 us -> 391 us  [the longest x1 256 us: take_blocks(): pl.pallas_call(functools.partial(pack_kernel, count), in_specs=[pl.BlockS...]
    unnamed x1, blocking collectives: 181 us -> 6.35 us
    all_to_all x2 -> x1, waiting for transfers between devices: 70.5 us -> 39.2 us  [exchange(): lax.all_to_all(shaped, 'req', split_axis=0, concat_axis=0, tiled=True)]
    all_to_all x2 -> x1, starting transfers between devices: 12 us -> 5.85 us  [exchange(): lax.all_to_all(shaped, 'req', split_axis=0, concat_axis=0, tiled=True)]
  transfers between devices with their start and end apart: 4 -> 7, of which waited for: 1 -> 1; matrix products, arithmetic and copies ran while one was open for 9% -> 7% of each run, Pallas kernels for 9% -> 77%
where the time goes in v2:
time: 517 us; the launch traced here: 516 us
  Pallas kernels  399 us (77%)
  waiting for transfers between devices  39.9 us (8%)
  matrix products  37.2 us (7%)
  between operations  14.8 us (3%)
  starting transfers between devices  8.41 us (2%)
  local copies, waits for them, and re-layouts  6.6 us (1%)
  blocking collectives  6.35 us (1%)
    pallas_call x1, Pallas kernels, take_blocks(): pl.pallas_call(functools.partial(pack_kernel, count), in_specs=[pl.BlockS...  256 us
    pallas_call x1, Pallas kernels, take_prompts(): pl.pallas_call(functools.partial(prompt_pack_kernel, parts, slots), in_sp...  129 us
    all_to_all x1, waiting for transfers between devices, exchange(): lax.all_to_all(shaped, 'req', split_axis=0, concat_axis=0, tiled=True)  39.2 us
    dot_general x4, matrix products, per_device(): jnp.dot(second_norm, w_in_full[part], preferred_element_type=jnp.float32)  16.7 us
  transfers between devices with their start and end apart: 7, of which 1 were waited for; matrix products, arithmetic and copies ran while one was open for 7% of the time, Pallas kernels for 77%

profile of v2, /device:TPU:0, one launch (start us, length us, event | category | flops | bytes accessed | tf_op | source)
XLA Modules:
  0.0 516.4 jit_solution(4740503834592951204)
XLA Ops:
  7.3 1.8 copy-done
  9.1 1.0 constant_dynamic-slice_fusion
  10.2 0.1 copy.29
  10.4 0.1 copy.30
  10.6 0.1 copy.28
  10.7 0.1 ne.50
  10.8 0.2 reduce_window_sum.11
  11.0 0.1 select_reduce_fusion
  11.2 0.6 reshape.154.ids_ref
  11.8 0.6 dynamic-slice.1
  13.1 0.2 dynamic-update-slice
  13.3 6.3 %all-reduce = s32[16]{0:T(128)S(1)} all-reduce(s32[16]{0:T(128)S(1)} %dynamic-update-slice), channel_id=2, replica_groups=mesh['req'=8,'grp'=4] {'grp'}, use_global_device_ids=true, to_apply=%add | all-reduce | flops 16 | bytes 128
  19.8 256.2 %shard_map.176 = bf16[32,64,2048]{2,1,0:T(8,128)(2,1)} custom-call(s32[32]{0:T(128)} %reshape.154.ids_ref, bf16[24,64,2048]{2,1,0:T(8,128)(2,1)} %source_ref.1), custom_call_target="tpu_custom_call" | custom-call | bytes 16777216 | tf_op jit(solution)/shard_map/pallas_call | solution.py:50
  276.0 5.8 %all-to-all-start = ((bf16[8,4,64,2048]{3,2,1,0:T(8,128)(2,1)}), bf16[8,4,64,2048]{3,2,1,0:T(8,128)(2,1)}, u32[]{:S(2)}, u32[]{:S(2)}) async-start(bf16[8,4,64,2048]{3,2,1,0:T(8,128)(2,1)} %bitcast.38), calls=%async_computation | async-start | bytes 16777216 | tf_op jit(solution)/shard_map/all_to_all | solution.py:263
  281.9 0.7 all-gather.7.cloned.1.call-update
  282.6 0.6 reshape.157.ids_ref
  283.5 0.2 convert_reduce_fusion
  283.7 0.6 multiply_add_fusion.ids_ref
  284.3 0.5 fusion.22
  284.7 0.3 fusion.24
  285.0 0.3 fusion.26
  285.3 0.8 convolution_minimum_fusion.reach_ref
  286.1 2.8 convolution_convert_fusion.2.value_ref
  288.9 0.3 convolution_convert_fusion
  289.3 0.7 convolution_convert_fusion.3.key_ref
  290.0 0.3 convolution_convert_fusion.1
  290.4 1.1 pad_maximum_fusion
  291.4 0.7 copy-done.11
  292.2 1.5 fusion.19.query_ref
  293.7 129.0 %shard_map.178 = (bf16[4,8,8,2048]{3,2,1,0:T(8,128)(2,1)}, bf16[4,8,8,2048]{3,2,1,0:T(8,128)(2,1)}, bf16[4,8,8,2048]{3,2,1,0:T(8,128)(2,1)}, bf16[4,8,8,2048]{3,2,1,0:T(8,128)(2,1)}) custom-call(s32[16]{0:T(128)} %reshape.157.ids_ref, bf16[8,24,8,2048]{3,2,1,0:T(8,128)(2,1)} %bitcast.39), custom_call_target="tpu_custom_call" | custom-call | bytes 8388608 | tf_op jit(solution)/shard_map/pallas_call | solution.py:86
  422.7 1.0 collective-permute-start.1
  423.7 1.4 collective-permute-start.2
  425.1 39.2 %all-to-all-done = bf16[8,4,64,2048]{3,2,1,0:T(8,128)(2,1)} async-done(((bf16[8,4,64,2048]{3,2,1,0:T(8,128)(2,1)}), bf16[8,4,64,2048]{3,2,1,0:T(8,128)(2,1)}, u32[]{:S(2)}, u32[]{:S(2)}) %all-to-all-start) | async-done | bytes 8388640 | tf_op jit(solution)/shard_map/all_to_all | solution.py:263
  464.3 7.9 %shard_map.177 = bf16[256,1024]{1,0:T(8,128)(2,1)} custom-call(s32[24]{0:T(128)} %multiply_add_fusion.ids_ref, s32[4]{0:T(128)} %lens_ref.1, bf16[256,1024]{1,0:T(8,128)(2,1)} %fusion.19.query_ref, bf16[256,1024]{1,0:T(8,128)(2,1)} %copy-done.3, bf16[256,1024]{1,0:T(8,128)(2,1)} %copy-done.2, f32[4,64,64]{2,1,0:T(8,128)} %convolution_minimum_fusion.reach_ref, ...), custom_call_target="tpu_custom_call" | custom-call | flops 1879048192 | bytes 9437184 | tf_op jit(solution)/shard_map/pallas_call | solution.py:158
  472.2 2.1 fusion.95
  474.4 0.3 multiply_reduce_fusion.2
  474.6 1.6 fusion.20.query_ref
  476.2 5.9 %shard_map.179 = bf16[256,1024]{1,0:T(8,128)(2,1)} custom-call(bf16[256,1024]{1,0:T(8,128)(2,1)} %fusion.20.query_ref, bf16[4,8,8,2048]{3,2,1,0:T(8,128)(2,1)} %get-tuple-element.14.rest_0_, bf16[4,8,8,2048]{3,2,1,0:T(8,128)(2,1)} %collective-permute-done.rest_1_, bf16[4,8,8,2048]{3,2,1,0:T(8,128)(2,1)} %collective-permute-done.1.rest_2_, ...), custom_call_target="tpu_custom_call" | custom-call | flops 1073741824 | bytes 5242880 | tf_op jit(solution)/shard_map/pallas_call | solution.py:206
  482.1 2.6 fusion.96
  484.7 0.3 multiply_reduce_fusion.1
  485.0 0.2 multiply_convert_fusion.1
  485.2 5.4 %fusion.29 = bf16[256,1024]{1,0:T(8,128)(2,1)} fusion(bf16[256,1024]{1,0:T(8,128)(2,1)S(1)} %multiply_convert_fusion.1, bf16[4096,1024]{1,0:T(8,128)(2,1)} %all-gather.11.cloned.1.call-done), kind=kOutput, calls=%fused_computation.46 | convolution fusion | flops 553910272 | bytes 3145728 | tf_op jit(solution)/shard_map/dot_general | solution.py:349
  490.7 3.8 fusion.32
  494.4 3.8 fusion.35
  498.2 3.7 fusion.38
  502.0 6.6 %fusion.97 = (f32[256]{0:T(256)S(1)}, f32[256,1024]{1,0:T(8,128)S(1)}) fusion(bf16[4096,1024]{1,0:T(8,128)(2,1)} %all-gather.7.cloned.1.call-done, bf16[256,1024]{1,0:T(8,128)(2,1)} %fusion.38, bf16[256,1024]{1,0:T(8,128)(2,1)} %fusion.35, bf16[256,1024]{1,0:T(8,128)(2,1)} %fusion.32, bf16[256,1024]{1,0:T(8,128)(2,1)} %fusion.29, ...), kind=kOutput, calls=%fused_computation.172 | convolution fusion | flops 2156658432 | bytes 12059648 | tf_op jit(solution)/shard_map/dot_general | solution.py:354
  508.6 0.3 multiply_reduce_fusion
  508.9 1.0 fusion.75
  (67 shorter events, 1.0 us)
Async XLA Ops:
  7.2 1.9 copy-start
  7.2 4.7 copy-start.16
  7.2 3.0 copy-start.7
  7.2 5.9 %copy-start.14 = (s32[4]{0:T(128)S(1)}, s32[4]{0:T(128)}, u32[]{:S(2)}) copy-start(s32[4]{0:T(128)} %param.24) | copy-start | bytes 52
  7.2 286.5 %all-gather.9.cloned.1.call-start = ((), (), s32[]{:S(2)}) async-start(), calls=%async_computation.2 | async-start | bytes 7077888 | tf_op jit(solution)/shard_map/all_gather | solution.py:226
  10.1 475.1 %all-gather.11.cloned.1.call-start = ((), (), s32[]{:S(2)}) async-start(), calls=%async_computation.3 | async-start | bytes 10485760 | tf_op jit(solution)/shard_map/all_gather | solution.py:308
  276.0 188.3 %all-to-all-start = ((bf16[8,4,64,2048]{3,2,1,0:T(8,128)(2,1)}), bf16[8,4,64,2048]{3,2,1,0:T(8,128)(2,1)}, u32[]{:S(2)}, u32[]{:S(2)}) async-start(bf16[8,4,64,2048]{3,2,1,0:T(8,128)(2,1)} %bitcast.38), calls=%async_computation | async-start | bytes 16777216 | tf_op jit(solution)/shard_map/all_to_all | solution.py:263
  281.8 1.4 copy-start.15
  281.8 2.4 copy-start.13
  281.9 4.3 copy-start.5
  281.9 220.1 %all-gather.7.cloned.1.call-start = ((), (), s32[]{:S(2)}) async-start(), calls=%async_computation.1 | async-start | bytes 10485760 | tf_op jit(solution)/shard_map/all_gather | solution.py:309
  284.7 4.2 copy-start.8
  286.1 3.1 copy-start.10
  288.9 1.1 copy-start.2
  290.0 3.7 copy-start.3
  290.0 2.2 copy-start.11
  422.7 53.5 %collective-permute-start = (bf16[4,8,8,2048]{3,2,1,0:T(8,128)(2,1)}, bf16[4,8,8,2048]{3,2,1,0:T(8,128)(2,1)}, u32[]{:S(2)}, u32[]{:S(2)}) collective-permute-start(bf16[4,8,8,2048]{3,2,1,0:T(8,128)(2,1)} %get-tuple-element.15), channel_id=1, source_target_pairs={{0,1},{1,2},{2,3},{3,0},{4,5},{5,6},{6,7},{7,4},{8,9},{9,10},{10,1... | collective-permute-start | bytes 3145736 | tf_op jit(solution)/shard_map/ppermute | solution.py:239
  422.7 53.5 %collective-permute-start.1 = (bf16[4,8,8,2048]{3,2,1,0:T(8,128)(2,1)}, bf16[4,8,8,2048]{3,2,1,0:T(8,128)(2,1)}, u32[]{:S(2)}, u32[]{:S(2)}) collective-permute-start(bf16[4,8,8,2048]{3,2,1,0:T(8,128)(2,1)} %get-tuple-element.16), channel_id=1, source_target_pairs={{0,2},{1,3},{2,0},{3,1},{4,6},{5,7},{6,4},{7,5},{8,10},{9,11},{10,... | collective-permute-start | bytes 3145736 | tf_op jit(solution)/shard_map/ppermute | solution.py:239
  423.7 52.5 %collective-permute-start.2 = (bf16[4,8,8,2048]{3,2,1,0:T(8,128)(2,1)}, bf16[4,8,8,2048]{3,2,1,0:T(8,128)(2,1)}, u32[]{:S(2)}, u32[]{:S(2)}) collective-permute-start(bf16[4,8,8,2048]{3,2,1,0:T(8,128)(2,1)} %get-tuple-element.17), channel_id=1, source_target_pairs={{0,3},{1,0},{2,1},{3,2},{4,7},{5,4},{6,5},{7,6},{8,11},{9,8},{10,9... | collective-permute-start | bytes 3145736 | tf_op jit(solution)/shard_map/ppermute | solution.py:239
  464.3 7.9 %copy-start.4 = (bf16[1024,1024]{1,0:T(8,128)(2,1)S(1)}, bf16[1024,1024]{1,0:T(8,128)(2,1)}, u32[]{:S(2)}) copy-start(bf16[1024,1024]{1,0:T(8,128)(2,1)} %param.29) | copy-start | bytes 6291460
  472.2 2.4 copy-start.12
  485.2 13.1 %copy-start.6 = (bf16[256,1024]{1,0:T(8,128)(2,1)}, bf16[256,1024]{1,0:T(8,128)(2,1)S(1)}, u32[]{:S(2)}) copy-start(bf16[256,1024]{1,0:T(8,128)(2,1)S(1)} %multiply_convert_fusion.1) | copy-start | bytes 1572868
  485.2 5.5 %copy-start.9 = (bf16[4096,1024]{1,0:T(8,128)(2,1)S(1)}, bf16[4096,1024]{1,0:T(8,128)(2,1)}, u32[]{:S(2)}) copy-start(bf16[4096,1024]{1,0:T(8,128)(2,1)} %all-gather.11.cloned.1.call-done) | copy-start | bytes 25165828
  502.0 7.9 %copy-start.1 = (bf16[24,32,2048]{2,1,0:T(8,128)(2,1)S(1)}, bf16[24,32,2048]{2,1,0:T(8,128)(2,1)}, u32[]{:S(2)}) copy-start(bf16[24,32,2048]{2,1,0:T(8,128)(2,1)} %param.25) | copy-start | bytes 9437188
Sparse Core Ops, SparseCore 0:
  10.2 101.7 all-gather.8
  276.1 58.8 all-gather.10
  336.6 58.2 all-gather.6

commit v3 on v2

--- a/solution.py
+++ b/solution.py
@@ -34,15 +34,30 @@
     return closure
 
 
-def pack_kernel(count, ids_ref, source_ref, out_ref, sems):
-    copies = [
-        pltpu.make_async_copy(source_ref.at[ids_ref[slot]], out_ref.at[slot], sems.at[slot])
-        for slot in range(count)
+VMEM_BYTES = 24 * 1024 * 1024
+
+
+def stream(sources, targets, held_ref, in_sems, out_sems):
+    loads = [
+        pltpu.make_async_copy(source, held_ref.at[slot], in_sems.at[slot])
+        for slot, source in enumerate(sources)
     ]
-    for copy in copies:
-        copy.start()
-    for copy in copies:
-        copy.wait()
+    stores = [
+        pltpu.make_async_copy(held_ref.at[slot], target, out_sems.at[slot])
+        for slot, target in enumerate(targets)
+    ]
+    for load in loads:
+        load.start()
+    for load, store in zip(loads, stores):
+        load.wait()
+        store.start()
+    for store in stores:
+        store.wait()
+
+
+def pack_kernel(count, ids_ref, source_ref, out_ref, held_ref, in_sems, out_sems):
+    sources = [source_ref.at[ids_ref[slot]] for slot in range(count)]
+    stream(sources, [out_ref.at[slot] for slot in range(count)], held_ref, in_sems, out_sems)
 
 
 def take_blocks(source, ids):
@@ -55,7 +70,12 @@
         ],
         out_specs=pl.BlockSpec(memory_space=pl.ANY),
         out_shape=jax.ShapeDtypeStruct((count,) + source.shape[1:], source.dtype),
-        scratch_shapes=[pltpu.SemaphoreType.DMA((count,))],
+        scratch_shapes=[
+            pltpu.VMEM((count,) + source.shape[1:], source.dtype),
+            pltpu.SemaphoreType.DMA((count,)),
+            pltpu.SemaphoreType.DMA((count,)),
+        ],
+        compiler_params=pltpu.CompilerParams(vmem_limit_bytes=VMEM_BYTES),
         cost_estimate=pl.CostEstimate(
             flops=0, bytes_accessed=4 * count * source[0].size, transcendentals=0
         ),
@@ -63,20 +83,11 @@
 
 
 def prompt_pack_kernel(parts, slots, ids_ref, source_ref, *rest):
-    out_refs, sems = rest[:parts], rest[parts]
-    copies = [
-        pltpu.make_async_copy(
-            source_ref.at[:, ids_ref[part * slots + slot]],
-            out_refs[part].at[slot],
-            sems.at[part * slots + slot],
-        )
-        for part in range(parts)
-        for slot in range(slots)
-    ]
-    for copy in copies:
-        copy.start()
-    for copy in copies:
-        copy.wait()
+    out_refs = rest[:parts]
+    held_ref, in_sems, out_sems = rest[parts:]
+    sources = [source_ref.at[:, ids_ref[place]] for place in range(parts * slots)]
+    targets = [out_refs[part].at[slot] for part in range(parts) for slot in range(slots)]
+    stream(sources, targets, held_ref, in_sems, out_sems)
 
 
 def take_prompts(source, ids, parts):
@@ -91,7 +102,12 @@
         ],
         out_specs=[pl.BlockSpec(memory_space=pl.ANY)] * parts,
         out_shape=[shape] * parts,
-        scratch_shapes=[pltpu.SemaphoreType.DMA((parts * slots,))],
+        scratch_shapes=[
+            pltpu.VMEM((parts * slots,) + shape.shape[1:], source.dtype),
+            pltpu.SemaphoreType.DMA((parts * slots,)),
+            pltpu.SemaphoreType.DMA((parts * slots,)),
+        ],
+        compiler_params=pltpu.CompilerParams(vmem_limit_bytes=VMEM_BYTES),
         cost_estimate=pl.CostEstimate(
             flops=0, bytes_accessed=4 * parts * shape.size, transcendentals=0
         ),

time: 517 us -> 427 us (0.83)
  Pallas kernels: 399 us -> 18.6 us
  waiting for transfers between devices: 39.9 us -> 320 us
  local copies, waits for them, and re-layouts: 6.6 us -> 15.3 us
    pallas_call x1, Pallas kernels: 256 us -> 2.54 us  [take_blocks(): pl.pallas_call(functools.partial(pack_kernel, count), in_specs=[pl.BlockS...]
    all_gather x1, waiting for transfers between devices: 0.01 us -> 209 us  [fetch_prompts(): return lax.all_gather(quarter, 'req', axis=0, tiled=False)]
    pallas_call x1, Pallas kernels: 129 us -> 2.38 us  [take_prompts(): pl.pallas_call(functools.partial(prompt_pack_kernel, parts, slots), in_sp...]
    ppermute x3, waiting for transfers between devices: 0.01 us -> 57.5 us  [trade_prompts(): arrived.append(lax.ppermute(packed[shift], 'grp', ring))]
    all_gather x1, waiting for transfers between devices: 0.01 us -> 33.6 us  [per_device(): w_out_full = lax.all_gather(w_out, 'grp', axis=0, tiled=True)]
    all_to_all x1, waiting for transfers between devices: 39.2 us -> 18.7 us  [exchange(): lax.all_to_all(shaped, 'req', split_axis=0, concat_axis=0, tiled=True)]
    unnamed x37 -> x47, local copies, waits for them, and re-layouts: 3.46 us -> 13.2 us
  transfers between devices with their start and end apart: 7 -> 7, of which waited for: 1 -> 6; matrix products, arithmetic and copies ran while one was open for 7% -> 9% of each run, Pallas kernels for 77% -> 4%
where the time goes in v3:
time: 427 us; the launch traced here: 426 us
  waiting for transfers between devices  320 us (75%)
  matrix products  37.9 us (9%)
  Pallas kernels  18.6 us (4%)
  local copies, waits for them, and re-layouts  15.3 us (4%)
  between operations  14.8 us (3%)
  starting transfers between devices  8.97 us (2%)
  blocking collectives  6.35 us (1%)
    all_gather x1, waiting for transfers between devices, fetch_prompts(): return lax.all_gather(quarter, 'req', axis=0, tiled=False)  209 us
    ppermute x3, waiting for transfers between devices, trade_prompts(): arrived.append(lax.ppermute(packed[shift], 'grp', ring))  57.5 us
    all_gather x1, waiting for transfers between devices, per_device(): w_out_full = lax.all_gather(w_out, 'grp', axis=0, tiled=True)  33.6 us
    all_to_all x1, waiting for transfers between devices, exchange(): lax.all_to_all(shaped, 'req', split_axis=0, concat_axis=0, tiled=True)  18.7 us
    dot_general x4, matrix products, per_device(): jnp.dot(second_norm, w_in_full[part], preferred_element_type=jnp.float32)  17.1 us
    unnamed x47, local copies, waits for them, and re-layouts  13.2 us
  transfers between devices with their start and end apart: 7, of which 6 were waited for; matrix products, arithmetic and copies ran while one was open for 9% of the time, Pallas kernels for 4%

profile of v3, /device:TPU:0, one launch (start us, length us, event | category | flops | bytes accessed | tf_op | source)
XLA Modules:
  0.0 426.0 jit_solution(14132685098994290894)
XLA Ops:
  7.3 1.8 copy-done
  9.1 1.0 constant_dynamic-slice_fusion
  11.3 0.6 dynamic-slice.1
  12.6 0.2 dynamic-update-slice
  12.8 6.3 %all-reduce = s32[16]{0:T(128)S(1)} all-reduce(s32[16]{0:T(128)S(1)} %dynamic-update-slice), channel_id=2, replica_groups=mesh['req'=8,'grp'=4] {'grp'}, use_global_device_ids=true, to_apply=%add | all-reduce | flops 16 | bytes 128
  19.3 3.3 copy-done.3
  22.6 2.5 shard_map.176
  25.1 3.2 copy-done.2
  28.4 5.9 %all-to-all-start = ((bf16[8,4,64,2048]{3,2,1,0:T(8,128)(2,1)}), bf16[8,4,64,2048]{3,2,1,0:T(8,128)(2,1)}, u32[]{:S(2)}, u32[]{:S(2)}) async-start(bf16[8,4,64,2048]{3,2,1,0:T(8,128)(2,1)} %bitcast.38), calls=%async_computation | async-start | bytes 16777216 | tf_op jit(solution)/shard_map/all_to_all | solution.py:279
  34.3 0.7 all-gather.7.cloned.1.call-update
  35.3 0.2 convert_reduce_fusion
  35.5 0.6 multiply_add_fusion.ids_ref
  36.1 0.5 fusion.22
  36.6 0.3 fusion.24
  36.9 0.3 fusion.26
  37.2 0.8 convolution_minimum_fusion.reach_ref
  38.0 2.4 convolution_convert_fusion.2.value_ref
  40.5 0.3 convolution_convert_fusion
  40.9 0.7 convolution_convert_fusion.3.key_ref
  41.6 0.3 convolution_convert_fusion.1
  41.9 1.1 pad_maximum_fusion
  43.0 0.8 copy-done.16
  43.8 1.5 fusion.19.query_ref
  45.3 209.3 %all-gather.9.cloned.1.call-done = bf16[192,8,2048]{2,1,0:T(8,128)(2,1)} async-done(((bf16[24,8,2048]{2,1,0:T(8,128)(2,1)}), bf16[192,8,2048]{2,1,0:T(8,128)(2,1)}) %all-gather.9.cloned.1.call-update) | async-done | bytes 6291472 | tf_op jit(solution)/shard_map/all_gather | solution.py:242
  254.6 2.8 copy-done.4
  257.4 2.4 shard_map.178
  259.9 1.5 collective-permute-start.1
  261.4 1.4 collective-permute-start.2
  262.8 18.7 %all-to-all-done = bf16[8,4,64,2048]{3,2,1,0:T(8,128)(2,1)} async-done(((bf16[8,4,64,2048]{3,2,1,0:T(8,128)(2,1)}), bf16[8,4,64,2048]{3,2,1,0:T(8,128)(2,1)}, u32[]{:S(2)}, u32[]{:S(2)}) %all-to-all-start) | async-done | bytes 8388640 | tf_op jit(solution)/shard_map/all_to_all | solution.py:279
  281.4 7.7 %shard_map.177 = bf16[256,1024]{1,0:T(8,128)(2,1)} custom-call(s32[24]{0:T(128)} %multiply_add_fusion.ids_ref, s32[4]{0:T(128)} %lens_ref.1, bf16[256,1024]{1,0:T(8,128)(2,1)} %fusion.19.query_ref, bf16[256,1024]{1,0:T(8,128)(2,1)} %copy-done.9, bf16[256,1024]{1,0:T(8,128)(2,1)} %copy-done.8, f32[4,64,64]{2,1,0:T(8,128)} %convolution_minimum_fusion.reach_ref, ...), custom_call_target="tpu_custom_call" | custom-call | flops 1879048192 | bytes 9437184 | tf_op jit(solution)/shard_map/pallas_call | solution.py:174
  289.2 2.8 fusion.95
  292.0 0.2 multiply_reduce_fusion.2
  292.3 1.6 fusion.20.query_ref
  293.9 10.5 %collective-permute-done.rest_1_ = bf16[4,8,8,2048]{3,2,1,0:T(8,128)(2,1)} collective-permute-done((bf16[4,8,8,2048]{3,2,1,0:T(8,128)(2,1)S(1)}, bf16[4,8,8,2048]{3,2,1,0:T(8,128)(2,1)}, u32[]{:S(2)}, u32[]{:S(2)}) %collective-permute-start) | collective-permute-done | bytes 1048608 | tf_op jit(solution)/shard_map/ppermute | solution.py:255
  304.3 2.6 collective-permute-done.1.rest_2_
  306.9 44.4 %collective-permute-done.2.rest_3_ = bf16[4,8,8,2048]{3,2,1,0:T(8,128)(2,1)} collective-permute-done((bf16[4,8,8,2048]{3,2,1,0:T(8,128)(2,1)}, bf16[4,8,8,2048]{3,2,1,0:T(8,128)(2,1)}, u32[]{:S(2)}, u32[]{:S(2)}) %collective-permute-start.2) | collective-permute-done | bytes 1048608 | tf_op jit(solution)/shard_map/ppermute | solution.py:255
  351.4 6.0 %shard_map.179 = bf16[256,1024]{1,0:T(8,128)(2,1)} custom-call(bf16[256,1024]{1,0:T(8,128)(2,1)} %fusion.20.query_ref, bf16[4,8,8,2048]{3,2,1,0:T(8,128)(2,1)} %copy-done.5, bf16[4,8,8,2048]{3,2,1,0:T(8,128)(2,1)} %collective-permute-done.rest_1_, bf16[4,8,8,2048]{3,2,1,0:T(8,128)(2,1)} %collective-permute-done.1.rest_2_, ...), custom_call_target="tpu_custom_call" | custom-call | flops 1073741824 | bytes 5242880 | tf_op jit(solution)/shard_map/pallas_call | solution.py:222
  357.4 2.6 fusion.96
  360.0 0.3 multiply_reduce_fusion.1
  360.5 5.8 %fusion.29 = bf16[256,1024]{1,0:T(8,128)(2,1)} fusion(bf16[256,1024]{1,0:T(8,128)(2,1)S(1)} %multiply_convert_fusion.1, bf16[4096,1024]{1,0:T(8,128)(2,1)} %all-gather.11.cloned.1.call-done), kind=kOutput, calls=%fused_computation.46 | convolution fusion | flops 553910272 | bytes 3145728 | tf_op jit(solution)/shard_map/dot_general | solution.py:365
  366.3 0.4 copy-done.14
  366.8 3.8 fusion.32
  370.5 3.8 fusion.35
  374.3 3.7 fusion.38
  378.0 33.6 %all-gather.7.cloned.1.call-done = bf16[4096,1024]{1,0:T(8,128)(2,1)} async-done(((bf16[1024,1024]{1,0:T(8,128)(2,1)}), bf16[4096,1024]{1,0:T(8,128)(2,1)}) %all-gather.7.cloned.1.call-update) | async-done | bytes 8388624 | tf_op jit(solution)/shard_map/all_gather | solution.py:325
  411.6 6.6 %fusion.97 = (f32[256]{0:T(256)S(1)}, f32[256,1024]{1,0:T(8,128)S(1)}) fusion(bf16[4096,1024]{1,0:T(8,128)(2,1)} %all-gather.7.cloned.1.call-done, bf16[256,1024]{1,0:T(8,128)(2,1)} %fusion.38, bf16[256,1024]{1,0:T(8,128)(2,1)} %fusion.35, bf16[256,1024]{1,0:T(8,128)(2,1)} %fusion.32, bf16[256,1024]{1,0:T(8,128)(2,1)} %fusion.29, ...), kind=kOutput, calls=%fused_computation.172 | convolution fusion | flops 2156658432 | bytes 12059648 | tf_op jit(solution)/shard_map/dot_general | solution.py:370
  418.2 0.3 multiply_reduce_fusion
  418.5 1.0 fusion.75
  (77 shorter events, 2.1 us)
Async XLA Ops:
  7.2 1.9 copy-start
  7.2 4.1 copy-start.21
  7.2 3.0 copy-start.12
  7.2 5.4 %copy-start.19 = (s32[4]{0:T(128)S(1)}, s32[4]{0:T(128)}, u32[]{:S(2)}) copy-start(s32[4]{0:T(128)} %param.24) | copy-start | bytes 52
  7.2 247.4 %all-gather.9.cloned.1.call-start = ((), (), s32[]{:S(2)}) async-start(), calls=%async_computation.2 | async-start | bytes 7077888 | tf_op jit(solution)/shard_map/all_gather | solution.py:242
  10.1 350.3 %all-gather.11.cloned.1.call-start = ((), (), s32[]{:S(2)}) async-start(), calls=%async_computation.3 | async-start | bytes 10485760 | tf_op jit(solution)/shard_map/all_gather | solution.py:324
  19.3 3.3 copy-start.3
  25.1 3.2 copy-start.2
  28.4 253.1 %all-to-all-start = ((bf16[8,4,64,2048]{3,2,1,0:T(8,128)(2,1)}), bf16[8,4,64,2048]{3,2,1,0:T(8,128)(2,1)}, u32[]{:S(2)}, u32[]{:S(2)}) async-start(bf16[8,4,64,2048]{3,2,1,0:T(8,128)(2,1)} %bitcast.38), calls=%async_computation | async-start | bytes 16777216 | tf_op jit(solution)/shard_map/all_to_all | solution.py:279
  34.2 0.9 copy-start.20
  34.2 1.9 copy-start.18
  34.2 3.8 copy-start.10
  34.2 377.4 %all-gather.7.cloned.1.call-start = ((), (), s32[]{:S(2)}) async-start(), calls=%async_computation.1 | async-start | bytes 10485760 | tf_op jit(solution)/shard_map/all_gather | solution.py:325
  36.6 3.9 copy-start.13
  38.0 2.8 copy-start.15
  40.5 1.1 copy-start.8
  41.6 3.7 copy-start.9
  41.6 2.2 copy-start.16
  254.6 2.8 copy-start.4
  259.8 29.4 %copy-start.5 = (bf16[4,8,8,2048]{3,2,1,0:T(8,128)(2,1)}, bf16[4,8,8,2048]{3,2,1,0:T(8,128)(2,1)S(1)}, u32[]{:S(2)}) copy-start(bf16[4,8,8,2048]{3,2,1,0:T(8,128)(2,1)S(1)} %get-tuple-element.14.rest_0_) | copy-start | bytes 3145732
  259.8 44.6 %collective-permute-start = (bf16[4,8,8,2048]{3,2,1,0:T(8,128)(2,1)S(1)}, bf16[4,8,8,2048]{3,2,1,0:T(8,128)(2,1)}, u32[]{:S(2)}, u32[]{:S(2)}) collective-permute-start(bf16[4,8,8,2048]{3,2,1,0:T(8,128)(2,1)S(1)} %get-tuple-element.15), channel_id=1, source_target_pairs={{0,1},{1,2},{2,3},{3,0},{4,5},{5,6},{6,7},{7,4},{8,9},{9,10},{10,1... | collective-permute-start | bytes 3145736 | tf_op jit(solution)/shard_map/ppermute | solution.py:255
  259.9 47.1 %collective-permute-start.1 = (bf16[4,8,8,2048]{3,2,1,0:T(8,128)(2,1)S(1)}, bf16[4,8,8,2048]{3,2,1,0:T(8,128)(2,1)}, u32[]{:S(2)}, u32[]{:S(2)}) collective-permute-start(bf16[4,8,8,2048]{3,2,1,0:T(8,128)(2,1)S(1)} %get-tuple-element.16), channel_id=1, source_target_pairs={{0,2},{1,3},{2,0},{3,1},{4,6},{5,7},{6,4},{7,5},{8,10},{9,11},{10,... | collective-permute-start | bytes 3145736 | tf_op jit(solution)/shard_map/ppermute | solution.py:255
  261.4 90.0 %collective-permute-start.2 = (bf16[4,8,8,2048]{3,2,1,0:T(8,128)(2,1)}, bf16[4,8,8,2048]{3,2,1,0:T(8,128)(2,1)}, u32[]{:S(2)}, u32[]{:S(2)}) collective-permute-start(bf16[4,8,8,2048]{3,2,1,0:T(8,128)(2,1)} %get-tuple-element.17), channel_id=1, source_target_pairs={{0,3},{1,0},{2,1},{3,2},{4,7},{5,4},{6,5},{7,6},{8,11},{9,8},{10,9... | collective-permute-start | bytes 3145736 | tf_op jit(solution)/shard_map/ppermute | solution.py:255
  289.2 3.1 copy-start.17
  292.0 1.9 copy-start.6
  351.4 6.0 %copy-start.7 = (f32[256,1024]{1,0:T(8,128)S(1)}, f32[256,1024]{1,0:T(8,128)}, u32[]{:S(2)}) copy-start(f32[256,1024]{1,0:T(8,128)} %copy-done.6) | copy-start | bytes 3145732
  360.4 13.9 %copy-start.11 = (bf16[256,1024]{1,0:T(8,128)(2,1)}, bf16[256,1024]{1,0:T(8,128)(2,1)S(1)}, u32[]{:S(2)}) copy-start(bf16[256,1024]{1,0:T(8,128)(2,1)S(1)} %multiply_convert_fusion.1) | copy-start | bytes 1572868
  360.5 6.3 %copy-start.14 = (bf16[4096,1024]{1,0:T(8,128)(2,1)S(1)}, bf16[4096,1024]{1,0:T(8,128)(2,1)}, u32[]{:S(2)}) copy-start(bf16[4096,1024]{1,0:T(8,128)(2,1)} %all-gather.11.cloned.1.call-done) | copy-start | bytes 25165828
  411.6 7.9 %copy-start.1 = (bf16[24,32,2048]{2,1,0:T(8,128)(2,1)S(1)}, bf16[24,32,2048]{2,1,0:T(8,128)(2,1)}, u32[]{:S(2)}) copy-start(bf16[24,32,2048]{2,1,0:T(8,128)(2,1)} %param.25) | copy-start | bytes 9437188
Sparse Core Ops, SparseCore 0:
  10.2 244.2 all-gather.8
  256.1 98.2 all-gather.10
  356.0 55.5 all-gather.6

commit v4 on v1

--- a/solution.py
+++ b/solution.py
@@ -1,3 +1,5 @@
+import functools
+
 import jax
 import jax.numpy as jnp
 from jax import lax
@@ -32,22 +34,48 @@
     return closure
 
 
-def copy_block(ids_ref, source_ref, out_ref):
-    out_ref[...] = source_ref[...]
+VMEM_BYTES = 24 * 1024 * 1024
+
+
+def stream(sources, targets, held_ref, in_sems, out_sems):
+    loads = [
+        pltpu.make_async_copy(source, held_ref.at[slot], in_sems.at[slot])
+        for slot, source in enumerate(sources)
+    ]
+    stores = [
+        pltpu.make_async_copy(held_ref.at[slot], target, out_sems.at[slot])
+        for slot, target in enumerate(targets)
+    ]
+    for load in loads:
+        load.start()
+    for load, store in zip(loads, stores):
+        load.wait()
+        store.start()
+    for store in stores:
+        store.wait()
+
+
+def pack_kernel(count, ids_ref, source_ref, out_ref, held_ref, in_sems, out_sems):
+    sources = [source_ref.at[ids_ref[slot]] for slot in range(count)]
+    stream(sources, [out_ref.at[slot] for slot in range(count)], held_ref, in_sems, out_sems)
 
 
 def take_blocks(source, ids):
     count = ids.shape[0]
-    block = (1,) + source.shape[1:]
     return pl.pallas_call(
-        copy_block,
-        grid_spec=pltpu.PrefetchScalarGridSpec(
-            num_scalar_prefetch=1,
-            grid=(count,),
-            in_specs=[pl.BlockSpec(block, lambda step, ids_ref: (ids_ref[step], 0, 0))],
-            out_specs=pl.BlockSpec(block, lambda step, ids_ref: (step, 0, 0)),
-        ),
+        functools.partial(pack_kernel, count),
+        in_specs=[
+            pl.BlockSpec(memory_space=pltpu.SMEM),
+            pl.BlockSpec(memory_space=pl.ANY),
+        ],
+        out_specs=pl.BlockSpec(memory_space=pl.ANY),
         out_shape=jax.ShapeDtypeStruct((count,) + source.shape[1:], source.dtype),
+        scratch_shapes=[
+            pltpu.VMEM((count,) + source.shape[1:], source.dtype),
+            pltpu.SemaphoreType.DMA((count,)),
+            pltpu.SemaphoreType.DMA((count,)),
+        ],
+        compiler_params=pltpu.CompilerParams(vmem_limit_bytes=VMEM_BYTES),
         cost_estimate=pl.CostEstimate(
             flops=0, bytes_accessed=4 * count * source[0].size, transcendentals=0
         ),
@@ -212,13 +240,14 @@
     scale = head_dim ** (-0.5)
     row_index = lax.axis_index("req")
     col_index = lax.axis_index("grp")
+    send_ids, page_ids = page_plan(page_table, kv_pool.shape[0], row_index)
     all_groups = lax.all_gather(prompt_group, "req", axis=0, tiled=True)
+    send_ids, all_groups = lax.optimization_barrier((send_ids, all_groups))
+    pages = exchange(take_blocks(kv_pool, send_ids), owners)
+    memory = exchange(take_blocks(memory_kv, all_groups), owners)
+    pages = pages.reshape((-1,) + kv_pool.shape[1:])
     w_in_full = lax.all_gather(w_in, "grp", axis=0, tiled=False)
     w_out_full = lax.all_gather(w_out, "grp", axis=0, tiled=True)
-    send_ids, page_ids = page_plan(page_table, kv_pool.shape[0], row_index)
-    pages = exchange(take_blocks(kv_pool, send_ids), owners)
-    pages = pages.reshape((-1,) + kv_pool.shape[1:])
-    memory = exchange(take_blocks(memory_kv, all_groups), owners)
 
     flat_rows = tokens.reshape(req_count * draft_len, model_width)
     query_rows = (jnp.dot(flat_rows, w_query, preferred_element_type=jnp.float32) * scale).astype(

time: 378 us -> 357 us (0.944)
  blocking collectives: 181 us -> 13.1 us
  waiting for transfers between devices: 71.9 us -> 234 us
  Pallas kernels: 52.1 us -> 29.5 us
  local copies, waits for them, and re-layouts: 3.09 us -> 13.7 us
    unnamed x1 -> x0, blocking collectives: 181 us -> none
    all_to_all x2, waiting for transfers between devices: 70.5 us -> 232 us  [exchange(): lax.all_to_all(shaped, 'req', split_axis=0, concat_axis=0, tiled=True)]
    pallas_call x2, Pallas kernels: 38.4 us -> 15.8 us  [take_blocks(): pl.pallas_call(functools.partial(pack_kernel, count), in_specs=[pl.BlockS...]
    optimization_barrier x0 -> x1, blocking collectives: none -> 13.1 us  [per_device(): send_ids, all_groups = lax.optimization_barrier((send_ids, all_groups))]
    unnamed x31 -> x35, local copies, waits for them, and re-layouts: 1.65 us -> 12.8 us
  transfers between devices with their start and end apart: 4 -> 4, of which waited for: 1 -> 2; matrix products, arithmetic and copies ran while one was open for 9% -> 9% of each run, Pallas kernels for 9% -> 8%
where the time goes in v4:
time: 357 us
  waiting for transfers between devices  234 us (66%)
  matrix products  35.9 us (10%)
  Pallas kernels  29.5 us (8%)
  between operations  15 us (4%)
  local copies, waits for them, and re-layouts  13.7 us (4%)
  blocking collectives  13.1 us (4%)
  starting transfers between devices  9.95 us (3%)
  other arithmetic  5.83 us (2%)
    all_to_all x2, waiting for transfers between devices, exchange(): lax.all_to_all(shaped, 'req', split_axis=0, concat_axis=0, tiled=True)  232 us
    dot_general x4, matrix products, per_device(): jnp.dot(second_norm, w_in_full[part], preferred_element_type=jnp.float32)  15.9 us
    pallas_call x2, Pallas kernels, take_blocks(): pl.pallas_call(functools.partial(pack_kernel, count), in_specs=[pl.BlockS...  15.8 us
    optimization_barrier x1, blocking collectives, per_device(): send_ids, all_groups = lax.optimization_barrier((send_ids, all_groups))  13.1 us
    unnamed x35, local copies, waits for them, and re-layouts  12.8 us
    all_to_all x2, starting transfers between devices, exchange(): lax.all_to_all(shaped, 'req', split_axis=0, concat_axis=0, tiled=True)  9.88 us
    pallas_call x1, Pallas kernels, self_attention(): pl.pallas_call(self_kernel, grid_spec=pltpu.PrefetchScalarGridSpec(num_sc...  7.72 us
  transfers between devices with their start and end apart: 4, of which 2 were waited for; matrix products, arithmetic and copies ran while one was open for 9% of the time, Pallas kernels for 8%

profile of v4, /device:TPU:0, one launch (start us, length us, event | category | flops | bytes accessed | tf_op | source)
XLA Modules:
  0.0 356.5 jit_solution(2658750068609496732)
XLA Ops:
  7.2 0.9 broadcast_remainder_fusion
  8.1 0.7 sign_compare_fusion
  9.2 0.1 copy.25
  9.4 0.2 reduce_window_sum.11
  9.6 0.1 select_reduce_fusion
  9.9 1.2 dynamic-slice.1
  11.8 0.9 dynamic-update-slice
  12.7 13.1 %all-reduce.ids_ref = s32[32]{0:T(128)S(1)} all-reduce(s32[32]{0:T(128)S(1)} %dynamic-update-slice), channel_id=1, replica_groups=mesh['req'=8,'grp'=4] {'req'}, use_global_device_ids=true, to_apply=%add | all-reduce | flops 32 | bytes 256 | tf_op jit(solution)/shard_map/optimization_barrier | solution.py:245
  25.7 2.8 copy-done.4
  28.5 2.5 shard_map.176
  31.1 3.2 copy-done.2
  34.3 5.0 %all-to-all-start = ((bf16[8,4,64,2048]{3,2,1,0:T(8,128)(2,1)}), bf16[8,4,64,2048]{3,2,1,0:T(8,128)(2,1)}, u32[]{:S(2)}, u32[]{:S(2)}) async-start(bf16[8,4,64,2048]{3,2,1,0:T(8,128)(2,1)} %bitcast.38), calls=%async_computation | async-start | bytes 16777216 | tf_op jit(solution)/shard_map/all_to_all | solution.py:215
  39.3 0.7 all-gather.6.cloned.1.call-update
  40.0 0.7 all-gather.4.cloned.1.call-update
  40.7 1.9 copy-done.5
  42.6 13.2 %shard_map.178 = bf16[32,32,2048]{2,1,0:T(8,128)(2,1)S(1)} custom-call(s32[32]{0:T(128)S(1)} %all-reduce.ids_ref, bf16[24,32,2048]{2,1,0:T(8,128)(2,1)S(1)} %copy-done.5), custom_call_target="tpu_custom_call" | custom-call | bytes 8388608 | tf_op jit(solution)/shard_map/pallas_call | solution.py:65
  55.8 2.0 copy-done.3
  57.9 161.8 %all-to-all-done = bf16[8,4,64,2048]{3,2,1,0:T(8,128)(2,1)} async-done(((bf16[8,4,64,2048]{3,2,1,0:T(8,128)(2,1)}), bf16[8,4,64,2048]{3,2,1,0:T(8,128)(2,1)}, u32[]{:S(2)}, u32[]{:S(2)}) %all-to-all-start) | async-done | bytes 8388640 | tf_op jit(solution)/shard_map/all_to_all | solution.py:215
  219.7 4.9 %all-to-all-start.1 = ((bf16[8,4,32,2048]{3,2,1,0:T(8,128)(2,1)}), bf16[8,4,32,2048]{3,2,1,0:T(8,128)(2,1)}, u32[]{:S(2)}, u32[]{:S(2)}) async-start(bf16[8,4,32,2048]{3,2,1,0:T(8,128)(2,1)} %bitcast.39), calls=%async_computation.1 | async-start | bytes 8388608 | tf_op jit(solution)/shard_map/all_to_all | solution.py:215
  224.9 0.2 convert_reduce_fusion
  225.0 0.6 multiply_add_fusion.ids_ref
  225.7 0.5 fusion.22
  226.1 0.3 fusion.24
  226.4 0.3 fusion.26
  226.7 0.8 convolution_minimum_fusion.reach_ref
  227.5 2.4 convolution_convert_fusion.2.value_ref
  230.0 0.3 convolution_convert_fusion
  230.4 0.7 convolution_convert_fusion.3.key_ref
  231.1 0.3 convolution_convert_fusion.1
  231.5 1.1 pad_maximum_fusion
  232.6 0.7 copy-done.12
  233.3 1.5 fusion.19.query_ref
  234.8 7.7 %shard_map.177 = bf16[256,1024]{1,0:T(8,128)(2,1)} custom-call(s32[24]{0:T(128)} %multiply_add_fusion.ids_ref, s32[4]{0:T(128)} %lens_ref.1, bf16[256,1024]{1,0:T(8,128)(2,1)} %fusion.19.query_ref, bf16[256,1024]{1,0:T(8,128)(2,1)} %copy-done.7, bf16[256,1024]{1,0:T(8,128)(2,1)} %copy-done.6, f32[4,64,64]{2,1,0:T(8,128)} %convolution_minimum_fusion.reach_ref, ...), custom_call_target="tpu_custom_call" | custom-call | flops 1879048192 | bytes 9437184 | tf_op jit(solution)/shard_map/pallas_call | solution.py:142
  242.6 2.1 fusion.93
  244.7 0.3 multiply_reduce_fusion.2
  245.0 1.6 fusion.20.query_ref
  246.6 70.4 %all-to-all-done.1.memory_ref = bf16[8,4,32,2048]{3,2,1,0:T(8,128)(2,1)} async-done(((bf16[8,4,32,2048]{3,2,1,0:T(8,128)(2,1)}), bf16[8,4,32,2048]{3,2,1,0:T(8,128)(2,1)}, u32[]{:S(2)}, u32[]{:S(2)}) %all-to-all-start.1) | async-done | bytes 4194336 | tf_op jit(solution)/shard_map/all_to_all | solution.py:215
  317.0 6.0 %shard_map.179 = bf16[256,1024]{1,0:T(8,128)(2,1)} custom-call(bf16[256,1024]{1,0:T(8,128)(2,1)} %fusion.20.query_ref, bf16[8,4,32,2048]{3,2,1,0:T(8,128)(2,1)} %all-to-all-done.1.memory_ref), custom_call_target="tpu_custom_call" | custom-call | flops 1073741824 | bytes 5242880 | tf_op jit(solution)/shard_map/pallas_call | solution.py:178
  323.0 2.6 fusion.94
  325.6 0.3 multiply_reduce_fusion.1
  325.8 0.2 multiply_convert_fusion.1
  326.0 4.6 %fusion.29 = bf16[256,1024]{1,0:T(8,128)(2,1)S(1)} fusion(bf16[256,1024]{1,0:T(8,128)(2,1)S(1)} %multiply_convert_fusion.1, bf16[4096,1024]{1,0:T(8,128)(2,1)} %all-gather.6.cloned.1.call-done), kind=kOutput, calls=%fused_computation.46 | convolution fusion | flops 553910272 | bytes 3145728 | tf_op jit(solution)/shard_map/dot_general | solution.py:290
  330.6 3.8 %fusion.32 = bf16[256,1024]{1,0:T(8,128)(2,1)} fusion(bf16[256,1024]{1,0:T(8,128)(2,1)S(1)} %multiply_convert_fusion.1, bf16[4096,1024]{1,0:T(8,128)(2,1)S(1)} %copy-done.10), kind=kOutput, calls=%fused_computation.49 | convolution fusion | flops 553910272 | bytes 3145728 | tf_op jit(solution)/shard_map/dot_general | solution.py:290
  334.4 3.8 %fusion.35 = bf16[256,1024]{1,0:T(8,128)(2,1)} fusion(bf16[256,1024]{1,0:T(8,128)(2,1)S(1)} %multiply_convert_fusion.1, bf16[4096,1024]{1,0:T(8,128)(2,1)S(1)} %copy-done.10), kind=kOutput, calls=%fused_computation.52 | convolution fusion | flops 553910272 | bytes 3145728 | tf_op jit(solution)/shard_map/dot_general | solution.py:290
  338.2 3.7 %fusion.38 = bf16[256,1024]{1,0:T(8,128)(2,1)} fusion(bf16[256,1024]{1,0:T(8,128)(2,1)S(1)} %multiply_convert_fusion.1, bf16[4096,1024]{1,0:T(8,128)(2,1)S(1)} %copy-done.10), kind=kOutput, calls=%fused_computation.55 | convolution fusion | flops 553910272 | bytes 3145728 | tf_op jit(solution)/shard_map/dot_general | solution.py:290
  342.0 6.4 %fusion.95 = (f32[256]{0:T(256)S(1)}, f32[256,1024]{1,0:T(8,128)S(1)}) fusion(bf16[4096,1024]{1,0:T(8,128)(2,1)} %all-gather.4.cloned.1.call-done, bf16[256,1024]{1,0:T(8,128)(2,1)} %fusion.38, bf16[256,1024]{1,0:T(8,128)(2,1)} %fusion.35, bf16[256,1024]{1,0:T(8,128)(2,1)} %fusion.32, bf16[256,1024]{1,0:T(8,128)(2,1)S(1)} %fusion.29, ...), kind=kOutput, calls=%fused_computation.167 | convolution fusion | flops 2156658432 | bytes 12059648 | tf_op jit(solution)/shard_map/dot_general | solution.py:295
  348.4 0.3 multiply_reduce_fusion
  348.7 1.0 fusion.75
  (53 shorter events, 1.1 us)
Async XLA Ops:
  7.2 235.4 %copy-start = (bf16[1024,1024]{1,0:T(8,128)(2,1)S(1)}, bf16[1024,1024]{1,0:T(8,128)(2,1)}, u32[]{:S(2)}) copy-start(bf16[1024,1024]{1,0:T(8,128)(2,1)} %param.29) | copy-start | bytes 6291460
  25.7 2.8 copy-start.4
  31.0 3.2 copy-start.2
  34.3 185.4 %all-to-all-start = ((bf16[8,4,64,2048]{3,2,1,0:T(8,128)(2,1)}), bf16[8,4,64,2048]{3,2,1,0:T(8,128)(2,1)}, u32[]{:S(2)}, u32[]{:S(2)}) async-start(bf16[8,4,64,2048]{3,2,1,0:T(8,128)(2,1)} %bitcast.38), calls=%async_computation | async-start | bytes 16777216 | tf_op jit(solution)/shard_map/all_to_all | solution.py:215
  39.2 286.8 %all-gather.6.cloned.1.call-start = ((), (), s32[]{:S(2)}) async-start(), calls=%async_computation.3 | async-start | bytes 10485760 | tf_op jit(solution)/shard_map/all_gather | solution.py:249
  40.0 302.0 %all-gather.4.cloned.1.call-start = ((), (), s32[]{:S(2)}) async-start(), calls=%async_computation.2 | async-start | bytes 10485760 | tf_op jit(solution)/shard_map/all_gather | solution.py:250
  40.7 1.9 copy-start.5
  55.8 2.0 copy-start.3
  219.7 4.9 %copy-start.15 = (s32[1,16]{1,0:T(1,128)S(1)}, s32[1,16]{1,0:T(1,128)}, u32[]{:S(2)}) copy-start(s32[1,16]{1,0:T(1,128)} %param.21) | copy-start | bytes 196
  219.7 6.0 %copy-start.14 = (s32[4,64]{1,0:T(4,128)S(1)}, s32[4,64]{1,0:T(4,128)}, u32[]{:S(2)}) copy-start(s32[4,64]{1,0:T(4,128)} %param.22) | copy-start | bytes 3076
  219.7 7.9 %copy-start.8 = (bf16[4,64,1024]{2,1,0:T(8,128)(2,1)S(1)}, bf16[4,64,1024]{2,1,0:T(8,128)(2,1)}, u32[]{:S(2)}) copy-start(bf16[4,64,1024]{2,1,0:T(8,128)(2,1)} %param.17) | copy-start | bytes 1572868
  219.7 97.3 %all-to-all-start.1 = ((bf16[8,4,32,2048]{3,2,1,0:T(8,128)(2,1)}), bf16[8,4,32,2048]{3,2,1,0:T(8,128)(2,1)}, u32[]{:S(2)}, u32[]{:S(2)}) async-start(bf16[8,4,32,2048]{3,2,1,0:T(8,128)(2,1)} %bitcast.39), calls=%async_computation.1 | async-start | bytes 8388608 | tf_op jit(solution)/shard_map/all_to_all | solution.py:215
  226.1 3.9 %copy-start.9 = (s32[4,64]{1,0:T(4,128)S(1)}, s32[4,64]{1,0:T(4,128)}, u32[]{:S(2)}) copy-start(s32[4,64]{1,0:T(4,128)} %param.23) | copy-start | bytes 3076
  227.5 2.8 copy-start.11
  230.0 1.1 copy-start.6
  231.1 3.7 %copy-start.7 = (bf16[256,1024]{1,0:T(8,128)(2,1)}, bf16[256,1024]{1,0:T(8,128)(2,1)S(1)}, u32[]{:S(2)}) copy-start(bf16[256,1024]{1,0:T(8,128)(2,1)S(1)} %convolution_convert_fusion.3.key_ref) | copy-start | bytes 1572868
  231.1 2.2 copy-start.12
  242.6 2.4 copy-start.13
  326.0 4.6 %copy-start.10 = (bf16[4096,1024]{1,0:T(8,128)(2,1)S(1)}, bf16[4096,1024]{1,0:T(8,128)(2,1)}, u32[]{:S(2)}) copy-start(bf16[4096,1024]{1,0:T(8,128)(2,1)} %all-gather.6.cloned.1.call-done) | copy-start | bytes 25165828
  342.0 7.7 %copy-start.1 = (bf16[1024,1024]{1,0:T(8,128)(2,1)S(1)}, bf16[1024,1024]{1,0:T(8,128)(2,1)}, u32[]{:S(2)}) copy-start(bf16[1024,1024]{1,0:T(8,128)(2,1)} %param.29) | copy-start | bytes 6291460
Sparse Core Ops, SparseCore 0:
  41.6 59.5 all-gather.5
  102.8 58.2 all-gather.3

commit v5 on v4

--- a/solution.py
+++ b/solution.py
@@ -246,7 +246,7 @@
     pages = exchange(take_blocks(kv_pool, send_ids), owners)
     memory = exchange(take_blocks(memory_kv, all_groups), owners)
     pages = pages.reshape((-1,) + kv_pool.shape[1:])
-    w_in_full = lax.all_gather(w_in, "grp", axis=0, tiled=False)
+    w_in_full = lax.all_gather(w_in, "grp", axis=1, tiled=True)
     w_out_full = lax.all_gather(w_out, "grp", axis=0, tiled=True)
 
     flat_rows = tokens.reshape(req_count * draft_len, model_width)
@@ -284,17 +284,10 @@
         first_norm.astype(jnp.float32)
         + jnp.dot(cross_mix, w_cross_output, preferred_element_type=jnp.float32)
     ).astype(jnp.bfloat16)
-    summed = jnp.zeros(second_norm.shape, jnp.float32)
-    hidden = [
-        jax.nn.gelu(
-            jnp.dot(second_norm, w_in_full[part], preferred_element_type=jnp.float32),
-            approximate=False,
-        ).astype(jnp.bfloat16)
-        for part in range(w_in_full.shape[0])
-    ]
-    summed = jnp.dot(
-        jnp.concatenate(hidden, axis=1), w_out_full, preferred_element_type=jnp.float32
-    )
+    hidden = jax.nn.gelu(
+        jnp.dot(second_norm, w_in_full, preferred_element_type=jnp.float32), approximate=False
+    ).astype(jnp.bfloat16)
+    summed = jnp.dot(hidden, w_out_full, preferred_element_type=jnp.float32)
     group_lengths = draft_lengths[0]
     own_counts = lax.dynamic_slice_in_dim(group_lengths, col_index * req_count, req_count, 0)
     live = (jnp.arange(draft_len, dtype=jnp.int32)[None, :] < own_counts[:, None]).reshape(

time: 357 us -> 356 us (level)
    dot_general x5 -> x1, matrix products: 22.3 us -> 19.1 us  [per_device(): summed = jnp.dot(hidden, w_out_full, preferred_element_type=jnp.float32)]
    unnamed x35 -> x37, local copies, waits for them, and re-layouts: 12.8 us -> 12.8 us
  transfers between devices with their start and end apart: 4 -> 4, of which waited for: 2 -> 2; matrix products, arithmetic and copies ran while one was open for 9% -> 6% of each run, Pallas kernels for 8% -> 8%
where the time goes in v5:
time: 356 us; the launch traced here: 355 us
  waiting for transfers between devices  234 us (66%)
  matrix products  33.9 us (10%)
  Pallas kernels  29.5 us (8%)
  between operations  15 us (4%)
  local copies, waits for them, and re-layouts  13.7 us (4%)
  blocking collectives  13.1 us (4%)
  starting transfers between devices  9.77 us (3%)
  other arithmetic  5.49 us (2%)
    all_to_all x2, waiting for transfers between devices, exchange(): lax.all_to_all(shaped, 'req', split_axis=0, concat_axis=0, tiled=True)  233 us
    dot_general x1, matrix products, per_device(): summed = jnp.dot(hidden, w_out_full, preferred_element_type=jnp.float32)  19.1 us
    pallas_call x2, Pallas kernels, take_blocks(): pl.pallas_call(functools.partial(pack_kernel, count), in_specs=[pl.BlockS...  15.8 us
    optimization_barrier x1, blocking collectives, per_device(): send_ids, all_groups = lax.optimization_barrier((send_ids, all_groups))  13.1 us
    unnamed x37, local copies, waits for them, and re-layouts  12.8 us
    all_to_all x2, starting transfers between devices, exchange(): lax.all_to_all(shaped, 'req', split_axis=0, concat_axis=0, tiled=True)  9.69 us
    pallas_call x1, Pallas kernels, self_attention(): pl.pallas_call(self_kernel, grid_spec=pltpu.PrefetchScalarGridSpec(num_sc...  7.73 us
  transfers between devices with their start and end apart: 4, of which 2 were waited for; matrix products, arithmetic and copies ran while one was open for 6% of the time, Pallas kernels for 8%

profile of v5, /device:TPU:0, one launch (start us, length us, event | category | flops | bytes accessed | tf_op | source)
XLA Modules:
  0.0 354.8 jit_solution(13902722181582524020)
XLA Ops:
  7.2 0.7 all-gather.3.cloned.1.call-update
  7.9 0.7 broadcast_remainder_fusion
  8.7 0.1 copy.26
  8.8 0.1 copy.27
  9.0 0.7 sign_compare_fusion
  9.8 0.1 copy.25
  9.9 0.1 ne.50
  10.0 0.2 reduce_window_sum.11
  10.2 0.1 select_reduce_fusion
  10.3 0.1 copy.28
  10.5 1.2 dynamic-slice.1
  12.4 0.9 dynamic-update-slice
  13.2 13.1 %all-reduce.ids_ref = s32[32]{0:T(128)S(1)} all-reduce(s32[32]{0:T(128)S(1)} %dynamic-update-slice), channel_id=1, replica_groups=mesh['req'=8,'grp'=4] {'req'}, use_global_device_ids=true, to_apply=%add | all-reduce | flops 32 | bytes 256 | tf_op jit(solution)/shard_map/optimization_barrier | solution.py:245
  26.3 2.8 copy-done.4
  29.1 2.5 shard_map.176
  31.6 3.2 copy-done.2
  34.8 4.9 %all-to-all-start = ((bf16[8,4,64,2048]{3,2,1,0:T(8,128)(2,1)}), bf16[8,4,64,2048]{3,2,1,0:T(8,128)(2,1)}, u32[]{:S(2)}, u32[]{:S(2)}) async-start(bf16[8,4,64,2048]{3,2,1,0:T(8,128)(2,1)} %bitcast.35), calls=%async_computation | async-start | bytes 16777216 | tf_op jit(solution)/shard_map/all_to_all | solution.py:215
  39.8 0.7 all-gather.5.cloned.1.call-update
  40.6 1.9 copy-done.5
  42.5 13.2 %shard_map.178 = bf16[32,32,2048]{2,1,0:T(8,128)(2,1)S(1)} custom-call(s32[32]{0:T(128)S(1)} %all-reduce.ids_ref, bf16[24,32,2048]{2,1,0:T(8,128)(2,1)S(1)} %copy-done.5), custom_call_target="tpu_custom_call" | custom-call | bytes 8388608 | tf_op jit(solution)/shard_map/pallas_call | solution.py:65
  55.7 2.0 copy-done.3
  57.8 163.1 %all-to-all-done = bf16[8,4,64,2048]{3,2,1,0:T(8,128)(2,1)} async-done(((bf16[8,4,64,2048]{3,2,1,0:T(8,128)(2,1)}), bf16[8,4,64,2048]{3,2,1,0:T(8,128)(2,1)}, u32[]{:S(2)}, u32[]{:S(2)}) %all-to-all-start) | async-done | bytes 8388640 | tf_op jit(solution)/shard_map/all_to_all | solution.py:215
  220.9 4.7 %all-to-all-start.1 = ((bf16[8,4,32,2048]{3,2,1,0:T(8,128)(2,1)}), bf16[8,4,32,2048]{3,2,1,0:T(8,128)(2,1)}, u32[]{:S(2)}, u32[]{:S(2)}) async-start(bf16[8,4,32,2048]{3,2,1,0:T(8,128)(2,1)} %bitcast.36), calls=%async_computation.1 | async-start | bytes 8388608 | tf_op jit(solution)/shard_map/all_to_all | solution.py:215
  225.8 0.1 lt.53
  225.9 0.2 convert_reduce_fusion
  226.1 0.6 multiply_add_fusion.ids_ref
  226.7 0.5 fusion.48
  227.1 0.3 fusion.50
  227.4 0.3 fusion.52
  227.7 0.8 convolution_minimum_fusion.reach_ref
  228.5 2.3 convolution_convert_fusion.2.value_ref
  230.9 0.3 convolution_convert_fusion
  231.3 2.2 convolution_convert_fusion.3.key_ref
  233.4 0.3 convolution_convert_fusion.1
  233.8 1.1 pad_maximum_fusion
  234.8 1.5 fusion.45.query_ref
  236.4 7.7 %shard_map.177 = bf16[256,1024]{1,0:T(8,128)(2,1)} custom-call(s32[24]{0:T(128)} %multiply_add_fusion.ids_ref, s32[4]{0:T(128)} %lens_ref.1, bf16[256,1024]{1,0:T(8,128)(2,1)} %fusion.45.query_ref, bf16[256,1024]{1,0:T(8,128)(2,1)} %copy-done.8, bf16[256,1024]{1,0:T(8,128)(2,1)} %copy-done.7, f32[4,64,64]{2,1,0:T(8,128)} %convolution_minimum_fusion.reach_ref, ...), custom_call_target="tpu_custom_call" | custom-call | flops 1879048192 | bytes 9437184 | tf_op jit(solution)/shard_map/pallas_call | solution.py:142
  244.1 2.1 fusion.101
  246.3 0.3 multiply_reduce_fusion.2
  246.5 1.6 fusion.46.query_ref
  248.1 69.9 %all-to-all-done.1.memory_ref = bf16[8,4,32,2048]{3,2,1,0:T(8,128)(2,1)} async-done(((bf16[8,4,32,2048]{3,2,1,0:T(8,128)(2,1)}), bf16[8,4,32,2048]{3,2,1,0:T(8,128)(2,1)}, u32[]{:S(2)}, u32[]{:S(2)}) %all-to-all-start.1) | async-done | bytes 4194336 | tf_op jit(solution)/shard_map/all_to_all | solution.py:215
  318.1 6.0 %shard_map.179 = bf16[256,1024]{1,0:T(8,128)(2,1)} custom-call(bf16[256,1024]{1,0:T(8,128)(2,1)} %fusion.46.query_ref, bf16[8,4,32,2048]{3,2,1,0:T(8,128)(2,1)} %all-to-all-done.1.memory_ref), custom_call_target="tpu_custom_call" | custom-call | flops 1073741824 | bytes 5242880 | tf_op jit(solution)/shard_map/pallas_call | solution.py:178
  324.1 2.6 fusion.102
  326.7 0.2 multiply_reduce_fusion.1
  327.0 0.7 copy-done.6
  327.6 19.1 %fusion.103 = (f32[256]{0:T(256)S(1)}, f32[256,1024]{1,0:T(8,128)S(1)}) fusion(bf16[4096,1024]{1,0:T(8,128)(2,1)} %all-gather.5.cloned.1.call-done, bf16[1024,4096]{1,0:T(8,128)(2,1)} %all-gather.3.cloned.1.call-done, f32[256,1024]{1,0:T(8,128)} %copy-done.6, f32[256]{0:T(256)S(1)} %add_rsqrt_fusion.1, f32[256]{0:T(256)S(1)} %broadcast_multiply_fusion.1), kind=kOutput, calls=%fused_computation.155 | convolution fusion | flops 4365484032 | bytes 18877440 | tf_op jit(solution)/shard_map/dot_general | solution.py:290
  346.7 0.3 multiply_reduce_fusion
  347.0 1.0 fusion.53
  (50 shorter events, 0.6 us)
Async XLA Ops:
  7.2 236.9 %copy-start = (bf16[1024,1024]{1,0:T(8,128)(2,1)S(1)}, bf16[1024,1024]{1,0:T(8,128)(2,1)}, u32[]{:S(2)}) copy-start(bf16[1024,1024]{1,0:T(8,128)(2,1)} %param.29) | copy-start | bytes 6291460
  7.2 319.8 %all-gather.3.cloned.1.call-start = ((), (), s32[]{:S(2)}) async-start(), calls=%async_computation.2 | async-start | bytes 10485760 | tf_op jit(solution)/shard_map/all_gather | solution.py:249
  26.3 2.8 copy-start.4
  31.6 3.2 copy-start.2
  34.8 186.0 %all-to-all-start = ((bf16[8,4,64,2048]{3,2,1,0:T(8,128)(2,1)}), bf16[8,4,64,2048]{3,2,1,0:T(8,128)(2,1)}, u32[]{:S(2)}, u32[]{:S(2)}) async-start(bf16[8,4,64,2048]{3,2,1,0:T(8,128)(2,1)} %bitcast.35), calls=%async_computation | async-start | bytes 16777216 | tf_op jit(solution)/shard_map/all_to_all | solution.py:215
  39.8 287.8 %all-gather.5.cloned.1.call-start = ((), (), s32[]{:S(2)}) async-start(), calls=%async_computation.3 | async-start | bytes 10485760 | tf_op jit(solution)/shard_map/all_gather | solution.py:250
  40.5 1.9 copy-start.5
  55.7 2.0 copy-start.3
  220.8 4.8 %copy-start.16 = (s32[1,16]{1,0:T(1,128)S(1)}, s32[1,16]{1,0:T(1,128)}, u32[]{:S(2)}) copy-start(s32[1,16]{1,0:T(1,128)} %param.21) | copy-start | bytes 196
  220.8 5.8 %copy-start.15 = (s32[4,64]{1,0:T(4,128)S(1)}, s32[4,64]{1,0:T(4,128)}, u32[]{:S(2)}) copy-start(s32[4,64]{1,0:T(4,128)} %param.22) | copy-start | bytes 3076
  220.9 7.7 %copy-start.9 = (bf16[4,64,1024]{2,1,0:T(8,128)(2,1)S(1)}, bf16[4,64,1024]{2,1,0:T(8,128)(2,1)}, u32[]{:S(2)}) copy-start(bf16[4,64,1024]{2,1,0:T(8,128)(2,1)} %param.17) | copy-start | bytes 1572868
  220.9 97.2 %all-to-all-start.1 = ((bf16[8,4,32,2048]{3,2,1,0:T(8,128)(2,1)}), bf16[8,4,32,2048]{3,2,1,0:T(8,128)(2,1)}, u32[]{:S(2)}, u32[]{:S(2)}) async-start(bf16[8,4,32,2048]{3,2,1,0:T(8,128)(2,1)} %bitcast.36), calls=%async_computation.1 | async-start | bytes 8388608 | tf_op jit(solution)/shard_map/all_to_all | solution.py:215
  225.6 5.3 %copy-start.11 = (s32[4,64]{1,0:T(4,128)S(1)}, s32[4,64]{1,0:T(4,128)}, u32[]{:S(2)}) copy-start(s32[4,64]{1,0:T(4,128)} %param.23) | copy-start | bytes 3076
  227.7 3.5 copy-start.12
  230.8 5.5 %copy-start.7 = (bf16[256,1024]{1,0:T(8,128)(2,1)}, bf16[256,1024]{1,0:T(8,128)(2,1)S(1)}, u32[]{:S(2)}) copy-start(bf16[256,1024]{1,0:T(8,128)(2,1)S(1)} %convolution_convert_fusion.2.value_ref) | copy-start | bytes 1572868
  230.9 4.0 %copy-start.10 = (bf16[4,64,1024]{2,1,0:T(8,128)(2,1)S(1)}, bf16[4,64,1024]{2,1,0:T(8,128)(2,1)}, u32[]{:S(2)}) copy-start(bf16[4,64,1024]{2,1,0:T(8,128)(2,1)} %param.17) | copy-start | bytes 1572868
  230.9 4.0 %copy-start.13 = (bf16[1024,1024]{1,0:T(8,128)(2,1)S(1)}, bf16[1024,1024]{1,0:T(8,128)(2,1)}, u32[]{:S(2)}) copy-start(bf16[1024,1024]{1,0:T(8,128)(2,1)} %param.26) | copy-start | bytes 6291460
  233.4 2.9 copy-start.8
  244.1 2.4 copy-start.14
  326.6 1.0 copy-start.6
  327.6 20.4 %copy-start.1 = (bf16[1024,1024]{1,0:T(8,128)(2,1)S(1)}, bf16[1024,1024]{1,0:T(8,128)(2,1)}, u32[]{:S(2)}) copy-start(bf16[1024,1024]{1,0:T(8,128)(2,1)} %param.29) | copy-start | bytes 6291460
Sparse Core Ops, SparseCore 0:
  9.6 60.9 all-gather.2
  72.2 58.2 all-gather.4
